TPU v7x, 32 devices: a whole 2x2x4 slice. The times are simulated.
32 devices in a mesh: dp: 8 (over z, x), seq: 4 (over y, core).
Axes of the slice: x: 2, y: 2, z: 4, core: 2. Of those that a mesh axis runs over, the one named last changes fastest.
Arguments:
- tokens: bfloat16 [2, 8, 1024, 2048], P(None, 'dp', 'seq'), may hold values from -6 to 6
- lengths: int32 [2, 8], P(None, 'dp'), may hold values from 256 to 1024, as said below
- cotangent: bfloat16 [2, 8, 1024, 2048], P(None, 'dp', 'seq'), may hold values from -6 to 6
- norm_gain: bfloat16 [2048], P(('dp', 'seq')), may hold values from 0.099609375 to 1.8984375
- in_weight: bfloat16 [2048, 8192], P(('dp', 'seq')), may hold values from -0.125 to 0.125
- conv_weight: bfloat16 [4, 4096], P(None, ('dp', 'seq')), may hold values from -3 to 3
- conv_bias: bfloat16 [4096], P(('dp', 'seq')), may hold values from -3 to 3
- x_weight: bfloat16 [4096, 160], P(('dp', 'seq')), may hold values from -0.09375 to 0.09375
- dt_weight: bfloat16 [128, 4096], P(None, ('dp', 'seq')), may hold values from -0.5 to 0.5
- dt_bias: bfloat16 [4096], P(('dp', 'seq')), may hold values from -8 to -2
- a_log: bfloat16 [16, 4096], P(None, ('dp', 'seq')), may hold values from -2 to 2.765625
- skip_d: bfloat16 [4096], P(('dp', 'seq')), may hold values from 0.5 to 2
- out_weight: bfloat16 [4096, 2048], P(('dp', 'seq')), may hold values from -0.25 to 0.25
Outputs:
- block_out: bfloat16 [2, 8, 1024, 2048], P(None, 'dp', 'seq')
- input_grad: bfloat16 [2, 8, 1024, 2048], P(None, 'dp', 'seq')
- grad_norm_gain: float32 [2048], P(('dp', 'seq'))
- grad_in_weight: float32 [2048, 8192], P(('dp', 'seq'))
- grad_conv_weight: float32 [4, 4096], P(None, ('dp', 'seq'))
- grad_conv_bias: float32 [4096], P(('dp', 'seq'))
- grad_x_weight: float32 [4096, 160], P(('dp', 'seq'))
- grad_dt_weight: float32 [128, 4096], P(None, ('dp', 'seq'))
- grad_dt_bias: float32 [4096], P(('dp', 'seq'))
- grad_a_log: float32 [16, 4096], P(None, ('dp', 'seq'))
- grad_skip_d: float32 [4096], P(('dp', 'seq'))
- grad_out_weight: float32 [4096, 2048], P(('dp', 'seq'))
Inputs may be any that keep to these rules, and one draw needn't show every extreme that they name: `lengths`: the number of leading positions of each slot that hold tokens; later positions are padding.
All inputs are finite; a program needn't handle non-finite values.
Results may differ from a plain program's by a relative error of at most 0.012.
Values may be sent and summed in bfloat16 or wider, within the bound.
No kernel may reach another device: no remote copies, remote signals or barrier semaphores. Data moves between devices by JAX's collectives and lax.ppermute only.
A program may use at most 320 MiB of HBM per device.

v0:
```python
import jax
import jax.numpy as jnp
from jax import lax
from jax.experimental import pallas as pl
from jax.experimental.pallas import tpu as pltpu
from jax.sharding import PartitionSpec as P

F32 = jnp.float32
BF16 = jnp.bfloat16
LOG2E = 1.4426950408889634
CHUNK = 128
KCONV = 4
EPSILON = 1e-05
UNROLL = 16


def softplus(v):
    e = jnp.exp(-jnp.abs(v))
    series = e * (1.0 + e * (-0.5 + e * (1.0 / 3.0 - 0.25 * e)))
    return jnp.maximum(v, 0.0) + jnp.where(e < 0.0078125, series, jnp.log(1.0 + e))


def tree(values):
    while len(values) > 1:
        values = [a + b for a, b in zip(values[0::2], values[1::2])]
    return values[0]


def widen(value, width):
    return jnp.concatenate([value] * (width // 128), axis=1) if width > 128 else value


def own_token(tokens, states):
    row = lax.broadcasted_iota(jnp.int32, (tokens, UNROLL * states), 0) % UNROLL
    return row == lax.broadcasted_iota(jnp.int32, (tokens, UNROLL * states), 1) // states


def diagonal(maps):
    states, tokens = maps.shape
    column = lax.broadcasted_iota(jnp.int32, (states, UNROLL * states), 1) % states
    repeat = (column == lax.broadcasted_iota(jnp.int32, (states, UNROLL * states), 0)).astype(BF16)
    every = lax.dot_general(maps.astype(BF16), repeat, (((0,), (0,)), ((), ())), preferred_element_type=F32)
    return jnp.where(own_token(tokens, states), every, 0.0).astype(BF16)


def stagger(maps, out):
    states, tokens = maps.shape
    for i in range(tokens // UNROLL):
        at = (i + 1) * states
        out[at:at + states, :] = maps if i == 0 else pltpu.roll(maps, tokens - i * UNROLL, 1)


def lane_block(maps, group, states):
    return maps[pl.ds(pl.multiple_of((group + 1) * states, states), states), :]


def column(block, r):
    return jnp.broadcast_to(block[:, r:r + 1], (block.shape[0], 128))


def scan_forward_kernel(order, lengths, proj_ref, x_ref, dtw_ref, dtb_ref, alog_ref, skip_ref, held_ref,
                        y_ref, start_ref, state, steps, drive, ins, outs, spread, seen, ysum, *, width, micro):
    length, inner = x_ref.shape
    states = state.shape[0]
    live = pl.program_id(0) * length < lengths[micro]

    @pl.when(pl.program_id(0) == 0)
    def _():
        state[...] = jnp.zeros_like(state)

    @pl.when(jnp.logical_not(live))
    def _():
        y_ref[...] = jnp.zeros_like(y_ref)
        start_ref[...] = jnp.zeros_like(start_ref)

    @pl.when(live)
    def _():
        start_ref[0] = state[...]
        xs = x_ref[...].astype(F32)
        pre = jnp.dot(proj_ref[0:length, :].astype(BF16), dtw_ref[...], preferred_element_type=F32) + dtb_ref[...]
        step = softplus(pre)
        steps[...] = step
        drive[...] = step * xs
        stagger(proj_ref[length:length + states, :], ins)
        outs[UNROLL:UNROLL + length, :] = diagonal(proj_ref[length + states:length + 2 * states, :])
        for g in range(inner // width):
            lanes = slice(g * width, (g + 1) * width)
            rate = -jnp.exp(alog_ref[:, lanes].astype(F32)) * LOG2E
            for r in range(UNROLL):
                spread[r * states:(r + 1) * states, :] = column(ins[states:2 * states, :], r)

            def settle(group, slot):
                rows = pl.ds(pl.multiple_of(group * UNROLL, UNROLL), UNROLL)
                ysum[rows, lanes] = jnp.dot(outs[rows, :], seen[slot], preferred_element_type=F32)

            def advance(group, h, slot):
                base = pl.multiple_of(group * UNROLL, UNROLL)
                block = lane_block(ins, group + 1, states)
                for r in range(UNROLL):
                    st = steps[pl.ds(base + r, 1), lanes]
                    dr = drive[pl.ds(base + r, 1), lanes]
                    row = slice(r * states, (r + 1) * states)
                    h = jnp.exp2(st * rate) * h + widen(spread[row, :], width) * dr
                    spread[row, :] = column(block, r)
                    seen[slot, row, :] = h.astype(BF16)
                return h

            def pair(i, h):
                settle(2 * i, 1)
                h = advance(2 * i, h, 0)
                settle(2 * i + 1, 0)
                return advance(2 * i + 1, h, 1)

            state[:, lanes] = lax.fori_loop(0, length // UNROLL // 2, pair, state[:, lanes])
            settle(length // UNROLL, 1)
        y_ref[...] = (ysum[UNROLL:UNROLL + length, :] + skip_ref[...] * xs).astype(y_ref.dtype)


def spec_nat(length, cols):
    return pl.BlockSpec((length, cols), lambda i, order, lengths: (i, 0))


def whole_spec(shape):
    return pl.BlockSpec(shape, lambda i, order, lengths: (0,) * len(shape))


def placed(per_piece, count, micro, micros, reverse=False):
    def index(i, order, lengths):
        at = count - 1 - i if reverse else i
        return ((order[at // per_piece] * micros + micro) * per_piece + at % per_piece, 0)
    return index


def scan_forward(order, lengths, proj, x, dtw, dtb, alog, skip, micro, micros, held, width=512):
    length, inner = x.shape
    count = length // CHUNK
    states = alog.shape[0]
    rank = dtw.shape[0]
    per_piece = count // order.shape[0]
    width = min(width, inner)
    first = held is None
    return pl.pallas_call(
        lambda *refs: scan_forward_kernel(*refs, width=width, micro=micro),
        grid_spec=pltpu.PrefetchScalarGridSpec(
            num_scalar_prefetch=2,
            grid=(count,),
            in_specs=[
                spec_nat(CHUNK + 2 * states, rank), spec_nat(CHUNK, inner),
                whole_spec((rank, inner)), whole_spec((1, inner)), whole_spec((states, inner)), whole_spec((1, inner)),
                pl.BlockSpec(memory_space=pl.ANY),
            ],
            out_specs=[
                pl.BlockSpec((CHUNK, inner), placed(per_piece, count, micro, micros)),
                pl.BlockSpec((1, states, inner), lambda i, order, lengths: (i, 0, 0)),
            ],
            scratch_shapes=[
                pltpu.VMEM((states, inner), F32),
                pltpu.VMEM((CHUNK, inner), F32),
                pltpu.VMEM((CHUNK, inner), F32),
                pltpu.VMEM(((CHUNK // UNROLL + 2) * states, 128), F32),
                pltpu.VMEM((CHUNK + UNROLL, UNROLL * states), BF16),
                pltpu.VMEM((UNROLL * states, 128), F32),
                pltpu.VMEM((2, UNROLL * states, width), BF16),
                pltpu.VMEM((CHUNK + UNROLL, inner), F32),
            ],
        ),
        out_shape=[
            jax.ShapeDtypeStruct((micros * length, inner), BF16),
            jax.ShapeDtypeStruct((count, states, inner), F32),
        ],
        input_output_aliases={} if first else {8: 0},
        name="scan_forward",
    )(order, lengths, proj, x, dtw, dtb, alog, skip, dtb if first else held)


def scan_backward_kernel(order, lengths, proj_ref, x_ref, sg_ref, start_ref, dtw_ref, dtb_ref, alog_ref, skip_ref,
                         pg_ref, xg_ref, gdtw_ref, gdtb_ref, galog_ref, gskip_ref,
                         adjoint, steps, drive, grads, ins, outs, inmap, spread, seen, turns, hist, fac, bsum, csum,
                         lamb, stepg, *,
                         width, micro):
    length, inner = x_ref.shape
    states = adjoint.shape[0]
    at = pl.num_programs(0) - 1 - pl.program_id(0)
    live = at * length < lengths[micro]

    @pl.when(pl.program_id(0) == 0)
    def _():
        adjoint[...] = jnp.zeros_like(adjoint)
        gdtw_ref[...] = jnp.zeros_like(gdtw_ref)
        gdtb_ref[...] = jnp.zeros_like(gdtb_ref)
        galog_ref[...] = jnp.zeros_like(galog_ref)
        gskip_ref[...] = jnp.zeros_like(gskip_ref)

    @pl.when(jnp.logical_not(live))
    def _():
        pg_ref[...] = jnp.zeros_like(pg_ref)
        xg_ref[...] = jnp.zeros_like(xg_ref)

    @pl.when(live)
    def _():
        low = proj_ref[0:length, :].astype(BF16)
        pre = jnp.dot(low, dtw_ref[...], preferred_element_type=F32) + dtb_ref[...]
        step = softplus(pre)
        steps[...] = step
        drive[0:length, :] = step * x_ref[...].astype(F32)
        grads[...] = sg_ref[...].astype(F32)
        stagger(proj_ref[length:length + states, :], ins)
        stagger(proj_ref[length + states:length + 2 * states, :], outs)
        inmap[0:length, :] = diagonal(proj_ref[length:length + states, :])
        count = length // UNROLL
        for g in range(inner // width):
            lanes = slice(g * width, (g + 1) * width)
            decay = -jnp.exp(alog_ref[:, lanes].astype(F32))
            rate = decay * LOG2E
            for r in range(UNROLL):
                spread[r * states:(r + 1) * states, :] = column(ins[states:2 * states, :], r)

            def settle_states(group, slot):
                given = pl.ds(pl.multiple_of(jnp.maximum(group - 1, 0) * UNROLL, UNROLL), UNROLL)
                rows = pl.ds(pl.multiple_of(group * UNROLL, UNROLL), UNROLL)
                total = lax.dot_general(sg_ref[given, lanes], seen[slot], (((1,), (1,)), ((), ())),
                                        preferred_element_type=F32)
                csum[rows, :] = total if g == 0 else csum[rows, :] + total

            def advance(group, h, slot):
                base = pl.multiple_of(group * UNROLL, UNROLL)
                block = lane_block(ins, group + 1, states)
                for r in range(UNROLL):
                    st = steps[pl.ds(base + r, 1), lanes]
                    dr = drive[pl.ds(base + r, 1), lanes]
                    at = pl.ds(pl.multiple_of((base + r) * states, states), states)
                    row = slice(r * states, (r + 1) * states)
                    hist[at, :] = h
                    a = jnp.exp2(st * rate)
                    fac[at, :] = a
                    h = a * h + widen(spread[row, :], width) * dr
                    spread[row, :] = column(block, r)
                    seen[slot, row, :] = h.astype(BF16)
                return h

            def pair(i, h):
                settle_states(2 * i, 1)
                h = advance(2 * i, h, 0)
                settle_states(2 * i + 1, 0)
                return advance(2 * i + 1, h, 1)

            lax.fori_loop(0, count // 2, pair, start_ref[0, :, lanes])
            settle_states(count, 1)
            for r in range(UNROLL):
                spread[r * states:(r + 1) * states, :] = column(outs[count * states:(count + 1) * states, :], r)

            def settle_adjoints(group, slot):
                rows = pl.ds(pl.multiple_of(group * UNROLL, UNROLL), UNROLL)
                lamb[rows, lanes] = jnp.dot(inmap[rows, :], seen[slot], preferred_element_type=F32)
                total = lax.dot_general(drive[rows, lanes].astype(BF16), seen[slot], (((1,), (1,)), ((), ())),
                                        preferred_element_type=F32)
                bsum[rows, :] = total if g == 0 else bsum[rows, :] + total

            def retreat(group, adj, dsum, slot):
                base = pl.multiple_of(group * UNROLL, UNROLL)
                block = lane_block(outs, group - 1, states)
                for r in reversed(range(UNROLL)):
                    st = steps[pl.ds(base + r, 1), lanes]
                    sg = grads[pl.ds(base + r, 1), lanes]
                    at = pl.ds(pl.multiple_of((base + r) * states, states), states)
                    row = slice(r * states, (r + 1) * states)
                    lam = adj + widen(spread[row, :], width) * sg
                    spread[row, :] = column(block, r)
                    seen[slot, row, :] = lam.astype(BF16)
                    adj = fac[at, :] * lam
                    w = adj * hist[at, :]
                    dsum = dsum + w * st
                    q = w * decay
                    q = q[0:8] + q[8:16]
                    for k in range(width // 128):
                        turns[slot, k, r * 8:(r + 1) * 8, :] = q[:, k * 128:(k + 1) * 128]
                for k in range(width // 128):
                    for q in range(0, UNROLL, 8):
                        stepg[pl.ds(base + q, 8), g * width + k * 128:g * width + (k + 1) * 128] = tree(
                            [turns[slot, k, pl.ds(q * 8 + n, 8, stride=8), :] for n in range(8)])
                return adj, dsum

            def back_pair(i, carry):
                top = count - 1 - 2 * i
                settle_adjoints(top + 1, 1)
                carry = retreat(top, *carry, 0)
                settle_adjoints(top, 0)
                return retreat(top - 1, *carry, 1)

            adj, dsum = lax.fori_loop(0, count // 2, back_pair, (adjoint[:, lanes], jnp.zeros((states, width), F32)))
            settle_adjoints(0, 1)
            adjoint[:, lanes] = adj
            galog_ref[:, lanes] += dsum * decay
        xs = x_ref[...].astype(F32)
        sg = grads[...]
        lam_b = lamb[0:length, :]
        low = proj_ref[0:length, :].astype(BF16)
        pre = jnp.dot(low, dtw_ref[...], preferred_element_type=F32) + dtb_ref[...]
        pre_grad = (stepg[0:length, :] + xs * lam_b) * jax.nn.sigmoid(pre)
        gdtb_ref[...] += jnp.sum(pre_grad, axis=0, keepdims=True)
        gskip_ref[...] += jnp.sum(sg * xs, axis=0, keepdims=True)
        xg_ref[...] = (steps[...] * lam_b + skip_ref[...] * sg).astype(xg_ref.dtype)
        pre_low = pre_grad.astype(BF16)
        gdtw_ref[...] += lax.dot_general(low, pre_low, (((0,), (0,)), ((), ())), preferred_element_type=F32)
        pg_ref[0:length, :] = lax.dot_general(pre_low, dtw_ref[...], (((1,), (1,)), ((), ())), preferred_element_type=F32)
        mine = own_token(length, states)
        state = lax.broadcasted_iota(jnp.int32, (states, UNROLL * states), 1) % states
        pick = (state == lax.broadcasted_iota(jnp.int32, (states, UNROLL * states), 0)).astype(BF16)
        for row, sums in ((length, bsum[0:length, :]), (length + states, csum[UNROLL:UNROLL + length, :])):
            pg_ref[row:row + states, :] = lax.dot_general(
                pick, jnp.where(mine, sums, 0.0).astype(BF16), (((1,), (1,)), ((), ())), preferred_element_type=F32)


def scan_backward(order, lengths, proj, x, sg, starts, dtw, dtb, alog, skip, micro, micros, width=512):
    length, inner = x.shape
    count = length // CHUNK
    states = alog.shape[0]
    rank = dtw.shape[0]
    per_piece = count // order.shape[0]
    width = min(width, inner)
    rev = lambda cols: pl.BlockSpec((CHUNK, cols), lambda i, order, lengths: (count - 1 - i, 0))
    return pl.pallas_call(
        lambda *refs: scan_backward_kernel(*refs, width=width, micro=micro),
        grid_spec=pltpu.PrefetchScalarGridSpec(
            num_scalar_prefetch=2,
            grid=(count,),
            in_specs=[
                pl.BlockSpec((CHUNK + 2 * states, rank), lambda i, order, lengths: (count - 1 - i, 0)), rev(inner),
                pl.BlockSpec((CHUNK, inner), placed(per_piece, count, micro, micros, True)),
                pl.BlockSpec((1, states, inner), lambda i, order, lengths: (count - 1 - i, 0, 0)),
                whole_spec((rank, inner)), whole_spec((1, inner)), whole_spec((states, inner)), whole_spec((1, inner)),
            ],
            out_specs=[
                pl.BlockSpec((CHUNK + 2 * states, rank), lambda i, order, lengths: (count - 1 - i, 0)),
                rev(inner),
                whole_spec((rank, inner)), whole_spec((1, inner)), whole_spec((states, inner)), whole_spec((1, inner)),
            ],
            scratch_shapes=[
                pltpu.VMEM((states, inner), F32),
                pltpu.VMEM((CHUNK, inner), F32),
                pltpu.VMEM((CHUNK + UNROLL, inner), F32),
                pltpu.VMEM((CHUNK, inner), F32),
                pltpu.VMEM(((CHUNK // UNROLL + 2) * states, 128), F32),
                pltpu.VMEM(((CHUNK // UNROLL + 2) * states, 128), F32),
                pltpu.VMEM((CHUNK + UNROLL, UNROLL * states), BF16),
                pltpu.VMEM((UNROLL * states, 128), F32),
                pltpu.VMEM((2, UNROLL * states, width), BF16),
                pltpu.VMEM((2, width // 128, 8 * UNROLL, 128), F32),
                pltpu.VMEM((CHUNK * states, width), F32),
                pltpu.VMEM((CHUNK * states, width), F32),
                pltpu.VMEM((CHUNK + UNROLL, UNROLL * states), F32),
                pltpu.VMEM((CHUNK + UNROLL, UNROLL * states), F32),
                pltpu.VMEM((CHUNK + UNROLL, inner), F32),
                pltpu.VMEM((CHUNK + UNROLL, inner), F32),
            ],
        ),
        out_shape=[
            jax.ShapeDtypeStruct((count * (CHUNK + 2 * states), rank), F32),
            jax.ShapeDtypeStruct((length, inner), BF16),
            jax.ShapeDtypeStruct((rank, inner), F32),
            jax.ShapeDtypeStruct((1, inner), F32),
            jax.ShapeDtypeStruct((states, inner), F32),
            jax.ShapeDtypeStruct((1, inner), F32),
        ],
        name="scan_backward",
    )(order, lengths, proj, x, sg, starts, dtw, dtb, alog, skip)


def conv_forward_kernel(order, lengths, *refs, peers, micro):
    pieces = refs[:peers]
    gain_ref, wb_ref, cw_ref, cb_ref, xw_ref, held_ref, normed_ref, branch_ref, x_ref, proj_ref, pad = refs[peers:]
    length, inner = x_ref.shape
    at = pl.program_id(0)

    @pl.when(at == 0)
    def _():
        pad[0:8, :] = jnp.zeros((8, inner), F32)

    live = at * length < lengths[micro]

    @pl.when(jnp.logical_not(live))
    def _():
        for ref in (normed_ref, branch_ref, x_ref, proj_ref):
            ref[...] = jnp.zeros_like(ref)

    for p in range(peers):
        @pl.when(jnp.logical_and(live, order[at] == p))
        def _():
            tokens = pieces[p][...].astype(F32)
            scale = lax.rsqrt(jnp.mean(tokens * tokens, axis=-1, keepdims=True) + EPSILON)
            normed_ref[...] = (tokens * scale * gain_ref[...]).astype(BF16)

    @pl.when(live)
    def _():
        groups = wb_ref.shape[0]
        deep = normed_ref.shape[1] // groups
        branch = sum(jnp.dot(normed_ref[:, d * deep:(d + 1) * deep], wb_ref[d, 0:deep, :], preferred_element_type=F32)
                     for d in range(groups)).astype(BF16)
        branch_ref[...] = branch
        pad[8:8 + length, :] = branch.astype(F32)
        pre = cb_ref[...] + sum(cw_ref[k:k + 1, :] * pad[5 + k:5 + k + length, :] for k in range(KCONV))
        x = (pre * jax.nn.sigmoid(pre)).astype(BF16)
        x_ref[...] = x
        rank = proj_ref.shape[1]
        low = lax.dot_general(x, xw_ref[0:rank, :], (((1,), (1,)), ((), ())), preferred_element_type=F32)
        maps = lax.dot_general(xw_ref[rank:, :], x, (((1,), (1,)), ((), ())), preferred_element_type=F32)
        rows = CHUNK + maps.shape[0]
        for k in range(length // CHUNK):
            proj_ref[k * rows:k * rows + CHUNK, :] = low[k * CHUNK:(k + 1) * CHUNK, :]
            proj_ref[k * rows + CHUNK:(k + 1) * rows, :] = maps[:, k * CHUNK:(k + 1) * CHUNK]
        pad[0:8, :] = pad[length:length + 8, :]


def conv_forward(order, lengths, pieces, gain, wb, cw, cb, xw, rank, micro, micros, held):
    peers = len(pieces)
    tokens, width = pieces[0].shape
    inner = wb.shape[2]
    cols = xw.shape[0]
    rows = tokens // CHUNK * (CHUNK + cols - rank)
    first = held is None
    return pl.pallas_call(
        lambda *refs: conv_forward_kernel(*refs, peers=peers, micro=micro),
        grid_spec=pltpu.PrefetchScalarGridSpec(
            num_scalar_prefetch=2,
            grid=(peers,),
            in_specs=[whole_spec((tokens, width))] * peers + [
                whole_spec((1, width)),
                whole_spec(wb.shape), whole_spec((KCONV, inner)), whole_spec((1, inner)), whole_spec((cols, inner)),
                pl.BlockSpec(memory_space=pl.ANY),
            ],
            out_specs=[
                pl.BlockSpec((tokens, width), placed(1, peers, micro, micros)),
                spec_nat(tokens, inner), spec_nat(tokens, inner), spec_nat(rows, rank),
            ],
            scratch_shapes=[pltpu.VMEM((tokens + 8, inner), F32)],
        ),
        out_shape=[
            jax.ShapeDtypeStruct((micros * peers * tokens, width), BF16),
            jax.ShapeDtypeStruct((peers * tokens, inner), BF16),
            jax.ShapeDtypeStruct((peers * tokens, inner), BF16),
            jax.ShapeDtypeStruct((peers * rows, rank), F32),
        ],
        input_output_aliases={} if first else {peers + 7: 0},
        name="conv_forward",
    )(order, lengths, *pieces, gain, wb, cw, cb, xw, gain if first else held)


def conv_backward_kernel(order, lengths, pg_ref, xg_ref, branch_ref, prev_ref, x_ref, cw_ref, cb_ref, xw_ref, held_ref,
                         mixed_ref, gxw_ref, gcb_ref, gcw_ref, pad, ahead, *, micro):
    length, inner = x_ref.shape

    @pl.when(pl.program_id(0) == 0)
    def _():
        ahead[length:length + 8, :] = jnp.zeros((8, inner), F32)
        gxw_ref[...] = jnp.zeros_like(gxw_ref)
        gcb_ref[...] = jnp.zeros_like(gcb_ref)
        gcw_ref[...] = jnp.zeros_like(gcw_ref)

    at = pl.num_programs(0) - 1 - pl.program_id(0)
    live = at * length < lengths[micro]

    @pl.when(jnp.logical_not(live))
    def _():
        mixed_ref[...] = jnp.zeros_like(mixed_ref)

    @pl.when(live)
    def _():
        earliest = pl.program_id(0) == pl.num_programs(0) - 1
        pad[0:8, :] = jnp.where(earliest, 0.0, prev_ref[...].astype(F32)[8:16, :])
        pad[8:8 + length, :] = branch_ref[...].astype(F32)
        pre = cb_ref[...] + sum(cw_ref[k:k + 1, :] * pad[5 + k:5 + k + length, :] for k in range(KCONV))
        sig = jax.nn.sigmoid(pre)
        rank = pg_ref.shape[1]
        rows = CHUNK + xw_ref.shape[0] - rank
        low, maps = [], []
        for k in range(length // CHUNK):
            low.append(pg_ref[k * rows:k * rows + CHUNK, :].astype(BF16))
            maps.append(pg_ref[k * rows + CHUNK:(k + 1) * rows, :].astype(BF16))
        low, maps = jnp.concatenate(low, axis=0), jnp.concatenate(maps, axis=1)
        grad = (jnp.dot(low, xw_ref[0:rank, :], preferred_element_type=F32)
                + lax.dot_general(maps, xw_ref[rank:, :], (((0,), (0,)), ((), ())), preferred_element_type=F32)
                + xg_ref[...].astype(F32))
        grad = grad * (sig * (1.0 + pre * (1.0 - sig)))
        ahead[0:length, :] = grad
        gcb_ref[...] += jnp.sum(grad, axis=0, keepdims=True)
        for k in range(KCONV):
            gcw_ref[k:k + 1, :] += jnp.sum(grad * pad[5 + k:5 + k + length, :], axis=0, keepdims=True)
        mixed = sum(cw_ref[k:k + 1, :] * ahead[3 - k:3 - k + length, :] for k in range(KCONV))
        mixed_ref[...] = mixed.astype(BF16)
        gxw_ref[0:rank, :] += lax.dot_general(low, x_ref[...], (((0,), (0,)), ((), ())), preferred_element_type=F32)
        gxw_ref[rank:, :] += jnp.dot(maps, x_ref[...], preferred_element_type=F32)
        ahead[length:length + 8, :] = ahead[0:8, :]


def conv_backward(order, lengths, pg, xg, branch, x, cw, cb, xw, micro, micros, held):
    length, inner = x.shape
    tokens = length // order.shape[0]
    count = length // tokens
    cols = xw.shape[0]
    first = held is None
    rank = pg.shape[1]
    rows = pg.shape[0] // count
    rev = lambda width: pl.BlockSpec((tokens, width), lambda i, order, lengths: (count - 1 - i, 0))
    return pl.pallas_call(
        lambda *refs: conv_backward_kernel(*refs, micro=micro),
        grid_spec=pltpu.PrefetchScalarGridSpec(
            num_scalar_prefetch=2,
            grid=(count,),
            in_specs=[
                pl.BlockSpec((rows, rank), lambda i, order, lengths: (count - 1 - i, 0)), rev(inner), rev(inner),
                pl.BlockSpec((16, inner), lambda i, order, lengths: (jnp.maximum((count - 1 - i) * (tokens // 16) - 1, 0), 0)),
                rev(inner),
                whole_spec((KCONV, inner)), whole_spec((1, inner)), whole_spec((cols, inner)),
                pl.BlockSpec(memory_space=pl.ANY),
            ],
            out_specs=[
                pl.BlockSpec((tokens, inner), placed(1, count, micro, micros, True)),
                whole_spec((cols, inner)), whole_spec((1, inner)), whole_spec((KCONV, inner)),
            ],
            scratch_shapes=[pltpu.VMEM((tokens + 8, inner), F32), pltpu.VMEM((tokens + 8, inner), F32)],
        ),
        out_shape=[
            jax.ShapeDtypeStruct((micros * length, inner), BF16),
            jax.ShapeDtypeStruct((cols, inner), F32),
            jax.ShapeDtypeStruct((1, inner), F32),
            jax.ShapeDtypeStruct((KCONV, inner), F32),
        ],
        input_output_aliases={} if first else {10: 0},
        name="conv_backward",
    )(order, lengths, pg, xg, branch, branch, x, cw, cb, xw, cb if first else held)


def partner(value, step):
    peers = lax.axis_size("seq")
    return lax.ppermute(value, "seq", [(i, i ^ step) for i in range(peers)])


def halvings():
    step = lax.axis_size("seq") // 2
    while step >= 1:
        yield step
        step //= 2


def reversed_bits(value, peers):
    out = value * 0
    step = 1
    while step < peers:
        out = out * 2 + (value // step) % 2
        step *= 2
    return out


def finish_piece(value):
    for step in reversed(list(halvings())[:-1]):
        half = value.shape[0] // 2
        value = value[:half].astype(F32) + partner(value[half:], step).astype(F32)
        value = value if step == lax.axis_size("seq") // 2 else value.astype(BF16)
    return value


def sum_over_pieces(value):
    for step in reversed(list(halvings())[:-1]):
        value = value.astype(F32) + partner(value, step).astype(F32)
        value = value if step == lax.axis_size("seq") // 2 else value.astype(BF16)
    return value


def sum_to_owner(whole):
    ranks = lax.axis_size("dp")
    me = lax.axis_index("dp")
    share = whole.shape[1] // ranks
    parts = jnp.stack([lax.dynamic_slice_in_dim(whole, (me ^ r) * share, share, 1) for r in range(ranks)]).astype(F32)
    step = 1
    while parts.shape[0] > 1:
        parts = parts.reshape((parts.shape[0] // 2, 2) + parts.shape[1:])
        given = parts[:, 1].astype(BF16)
        other = lax.ppermute(given, "dp", [(i, i ^ step) for i in range(ranks)])
        parts = parts[:, 0] + other.astype(F32)
        step *= 2
    return parts[0]


def dot(left, right, dims, kind=F32):
    return lax.dot_general(left, right, (dims, ((), ())), preferred_element_type=kind)


def body(tokens, lengths, cotangent, norm_gain, in_weight, conv_weight, conv_bias, x_weight, dt_weight,
         dt_bias, a_log, skip_d, out_weight):
    micros, slots, piece, width = tokens.shape
    peers, groups = lax.axis_size("seq"), lax.axis_size("dp")
    me = lax.axis_index("seq")
    share = conv_bias.shape[0]
    inner = share * groups
    rows = in_weight.shape[0]
    rank = dt_weight.shape[0]
    states = a_log.shape[0]
    cols = x_weight.shape[1]
    length = piece * peers
    order = reversed_bits(jnp.arange(peers, dtype=jnp.int32) ^ me, peers)
    tokens, cotangent = tokens[:, 0], cotangent[:, 0]
    held = lengths[:, 0]

    gain_part = norm_gain
    for step in halvings():
        gain_part = jnp.concatenate([gain_part, partner(gain_part, step)])
    gain_part = gain_part.reshape(peers, rows)
    gain_part = jnp.concatenate([lax.dynamic_slice_in_dim(gain_part, order[q], 1) for q in range(peers)])
    gain_rows = peers * rows // share
    small = jnp.concatenate([
        a_log, conv_weight, conv_bias[None], dt_bias[None], skip_d[None], gain_part.reshape(gain_rows, share),
        jnp.zeros((states - KCONV - 3 - gain_rows, share), BF16), dt_weight, x_weight.T], axis=0)
    packed = small.shape[0]

    def mine(half):
        own = half.reshape(rows, groups, peers, share).transpose(2, 0, 1, 3).reshape(peers * rows, inner)
        return lax.all_to_all(own, "seq", split_axis=0, concat_axis=0, tiled=True)

    first = jnp.concatenate([mine(in_weight[:, :inner * peers]), small.reshape(-1, inner)], axis=0)
    first = lax.all_gather(first, "dp", axis=0, tiled=False)
    pieces = [[tokens[m]] for m in range(micros)]
    for step in halvings():
        for m in range(micros):
            pieces[m] = pieces[m] + [partner(part, step) for part in pieces[m]]
    late, pieces = lax.optimization_barrier((in_weight[:, inner * peers:], pieces))
    wg = lax.all_gather(mine(late), "dp", axis=0, tiled=True)
    wo = lax.all_gather(out_weight, "dp", axis=0, tiled=True)
    small = first[:, peers * rows:].reshape(groups, packed, share)
    at = states + KCONV + 3
    gain = small[:, at:at + gain_rows].reshape(1, width).astype(F32)
    small = jnp.concatenate([small[d] for d in range(groups)], axis=1)
    alog = small[0:states]
    at = states
    cw = small[at:at + KCONV].astype(F32)
    cb = small[at + KCONV:at + KCONV + 1].astype(F32)
    dtb = small[at + KCONV + 1:at + KCONV + 2].astype(F32)
    skip = small[at + KCONV + 2:at + KCONV + 3].astype(F32)
    dtw = small[2 * states:2 * states + rank]
    xw = small[2 * states + rank:]

    positions = me * piece + jnp.arange(piece, dtype=jnp.int32)
    valid = (positions[None, :] < lengths).astype(F32)[..., None]
    own_grad = (valid * cotangent.astype(F32)).astype(BF16)
    own_grad, pieces = lax.optimization_barrier((own_grad, pieces))
    grads = [own_grad]
    for step in list(halvings())[:-1]:
        grads = grads + [partner(part, step) for part in grads]
    convs, normed = [], None
    for m in range(micros):
        normed, branch, x, proj = conv_forward(order, held, pieces[m], gain, first, cw, cb, xw, rank, m, micros, normed)
        proj = (proj + partner(proj, 1)).astype(BF16)
        if m + 1 < micros:
            proj, pieces[m + 1], grads = lax.optimization_barrier((proj, pieces[m + 1], grads))
        convs.append((branch, x, sum_over_pieces(proj)))
    grads = grads + [partner(part, 1) for part in grads]
    y, starts = None, []
    for m in range(micros):
        y, start = scan_forward(order, held, convs[m][2], convs[m][1], dtw, dtb, alog, skip, m, micros, y)
        starts.append(start)
    normed, y = lax.optimization_barrier((normed, y))
    gate = dot(normed, wg, ((1,), (0,)))
    sig = jax.nn.sigmoid(gate)
    yf = y.astype(F32)
    gated = (yf * gate * sig).astype(BF16)
    out_grad = jnp.concatenate(grads, axis=0).reshape(micros * length, width)
    gwo = dot(gated, out_grad, ((0,), (0,)), BF16)
    gwo, gated, out_grad = lax.optimization_barrier((gwo, gated, out_grad))
    gg = dot(out_grad, wo, ((1,), (1,)))
    sg = (gg * gate * sig).astype(BF16)
    gate_grad = (gg * yf * sig * (1.0 + gate * (1.0 - sig))).astype(BF16)
    half = micros * length // 2
    given = dot(gated[half:], wo, ((1,), (0,)), BF16)
    kept = dot(gated[:half], wo, ((1,), (0,)), BF16)
    given, kept, gate_grad = lax.optimization_barrier((given, kept, gate_grad))
    gwg = dot(normed, gate_grad, ((0,), (0,)), BF16)
    added = (kept.astype(F32) + partner(given, 1).astype(F32)).astype(BF16)
    gwg, sg, added = lax.optimization_barrier((gwg, sg, added))
    added = finish_piece(added)
    gwo = lax.psum_scatter(gwo, "dp", scatter_dimension=0, tiled=True)
    gwg = lax.psum_scatter(gwg, "dp", scatter_dimension=0, tiled=True)
    gwg = lax.all_to_all(gwg, "seq", split_axis=0, concat_axis=0, tiled=True)
    backs = []
    for m in range(micros):
        given = sg
        if m == micros - 1:
            given, gwo, added = lax.optimization_barrier((given, gwo, added))
            result = (valid * (tokens.astype(F32) + added.reshape(micros, piece, width))).astype(BF16)
        backs.append(list(scan_backward(
            order, held, convs[m][2], convs[m][1], given, starts[m], dtw, dtb, alog, skip, m, micros)))
        backs[m][0] = (backs[m][0] + partner(backs[m][0], 1)).astype(BF16)
        if m + 1 < micros:
            backs[m][0] = sum_over_pieces(backs[m][0])
    for m in range(micros - 1):
        backs[m][0], backs[-1][1] = lax.optimization_barrier((backs[m][0], backs[-1][1]))
    mixed, totals = None, None
    for m in range(micros):
        pg, xg, gdtw, gdtb, galog, gskip = backs[m]
        if m == micros - 1:
            pg, mixed, gate_grad = lax.optimization_barrier((pg, mixed, gate_grad))
            pg = sum_over_pieces(pg)
            early = dot(gate_grad, wg, ((1,), (1,)))
            pg, early = lax.optimization_barrier((pg, early))
        mixed, gxw, gcb, gcw = conv_backward(
            order, held, pg, xg, convs[m][0], convs[m][1], cw, cb, xw, m, micros, mixed)
        part = [galog, gcw, gcb, gdtb, gskip, gdtw, gxw]
        totals = part if totals is None else [a + b for a, b in zip(totals, part)]
    gwb = dot(normed, mixed, ((0,), (0,)), BF16)
    gwb, totals, mixed = lax.optimization_barrier((gwb, totals, mixed))
    gwb = lax.psum_scatter(gwb, "dp", scatter_dimension=0, tiled=True)
    gsmall = sum_to_owner(jnp.concatenate(totals, axis=0))
    wb = first[:, :peers * rows].reshape(width, inner)
    w = (early + dot(mixed, wb, ((1,), (1,)))).astype(BF16)
    w = finish_piece((w[:half].astype(F32) + partner(w[half:], 1).astype(F32)).astype(BF16)).reshape(micros, piece, width)
    w, gwb, gsmall, gwg = lax.optimization_barrier((w, gwb, gsmall, gwg))
    w = w * gain
    inputs = tokens.astype(F32)
    scale = lax.rsqrt(jnp.mean(inputs * inputs, axis=-1, keepdims=True) + EPSILON)
    input_grad = (own_grad.astype(F32) + scale * w - inputs * (scale * scale * scale)
                  * jnp.mean(w * inputs, axis=-1, keepdims=True)).astype(BF16)
    gwb = lax.all_to_all(gwb, "seq", split_axis=0, concat_axis=0, tiled=True)
    spread = lambda g: g.astype(F32).reshape(peers, rows, groups, share).transpose(1, 2, 0, 3).reshape(rows, inner * peers)
    total = jnp.concatenate([spread(gwb), spread(gwg)], axis=1)
    g_gain = jnp.sum(in_weight.astype(F32) * total, axis=1) / norm_gain.astype(F32)
    pieces, at = [], 0
    for count in (states, KCONV, 1, 1, 1, rank, cols):
        pieces.append(gsmall[at:at + count])
        at += count
    galog, gcw, gcb, gdtb, gskip, gdtw, gxw = pieces
    return (
        result[:, None], input_grad[:, None], g_gain, total, gcw, gcb[0], gxw.T, gdtw, gdtb[0], galog, gskip[0],
        gwo.astype(F32),
    )


def solution(mesh):
    placed = (
        P(None, "dp", "seq", None),
        P(None, "dp"),
        P(None, "dp", "seq", None),
        P(("dp", "seq")),
        P(("dp", "seq"), None),
        P(None, ("dp", "seq")),
        P(("dp", "seq")),
        P(("dp", "seq"), None),
        P(None, ("dp", "seq")),
        P(("dp", "seq")),
        P(None, ("dp", "seq")),
        P(("dp", "seq")),
        P(("dp", "seq"), None),
    )
    return jax.shard_map(
        body,
        mesh=mesh,
        in_specs=placed,
        out_specs=(
            P(None, "dp", "seq", None),
            P(None, "dp", "seq", None),
            P(("dp", "seq")),
            P(("dp", "seq"), None),
            P(None, ("dp", "seq")),
            P(("dp", "seq")),
            P(("dp", "seq"), None),
            P(None, ("dp", "seq")),
            P(("dp", "seq")),
            P(None, ("dp", "seq")),
            P(("dp", "seq")),
            P(("dp", "seq"), None),
        ),
        check_vma=False,
    )
```

profile of v0, /device:TPU:0, one launch (start us, length us, event | category | flops | bytes accessed | tf_op | source)
XLA Modules:
  0.0 680.4 jit_solution(18279704250364613376)
XLA Ops:
  30.7 23.5 %collective-permute-done.3.refs_3_ = bf16[256,2048]{1,0:T(8,128)(2,1)S(1)} collective-permute-done((bf16[256,2048]{1,0:T(8,128)(2,1)S(1)}, bf16[256,2048]{1,0:T(8,128)(2,1)S(1)}, u32[]{:S(2)}, u32[]{:S(2)}) %collective-permute-start.3) | collective-permute-done | bytes 1048608 | tf_op jit(solution)/shard_map/ppermute | solution.py:535
  54.2 21.8 %collective-permute-done.refs_3_ = bf16[256,2048]{1,0:T(8,128)(2,1)S(1)} collective-permute-done((bf16[256,2048]{1,0:T(8,128)(2,1)S(1)}, bf16[256,2048]{1,0:T(8,128)(2,1)S(1)}, u32[]{:S(2)}, u32[]{:S(2)}) %collective-permute-start) | collective-permute-done | bytes 1048608 | tf_op jit(solution)/shard_map/ppermute | solution.py:535
  81.4 11.9 %all_to_all.45 = bf16[4,64,1024]{2,1,0:T(8,128)(2,1)} all-to-all(bf16[4,64,1024]{2,1,0:T(8,128)(2,1)S(1)} %all_to_all.33), channel_id=1, replica_groups=mesh['dp'=8,'seq'=4] {'seq'}, dimensions={0} | all-to-all | bytes 1048576 | tf_op jit(solution)/shard_map/all_to_all | solution.py:617
  96.2 14.1 %all-gather.9.cloned.1.call-done = bf16[2368,1024]{1,0:T(8,128)(2,1)} async-done(((bf16[296,1024]{1,0:T(8,128)(2,1)}), bf16[2368,1024]{1,0:T(8,128)(2,1)}) %all-gather.9.cloned.1.call-update) | async-done | bytes 4849680 | tf_op jit(solution)/shard_map/all_gather | solution.py:620
  119.2 12.6 %conv_forward.2 = (bf16[2048,2048]{1,0:T(8,128)(2,1)}, bf16[1024,1024]{1,0:T(8,128)(2,1)}, bf16[1024,1024]{1,0:T(8,128)(2,1)}, f32[1280,128]{1,0:T(8,128)}) custom-call(s32[4]{0:T(128)} %copy-done.26, s32[2]{0:T(128)} %bitcast.186, bf16[256,2048]{1,0:T(8,128)(2,1)} %copy-done.12, bf16[256,2048]{1,0:T(8,128)(2,1)} %copy-done.14, ...), custom_call_target="tpu_custom_call" | custom-call | tf_op jit(solution)/shard_map/conv_forward/pallas_call | solution.py:421
  143.3 12.8 %conv_forward.3 = (bf16[2048,2048]{1,0:T(8,128)(2,1)}, bf16[1024,1024]{1,0:T(8,128)(2,1)}, bf16[1024,1024]{1,0:T(8,128)(2,1)}, f32[1280,128]{1,0:T(8,128)}) custom-call(s32[4]{0:T(128)} %copy-done.26, s32[2]{0:T(128)} %bitcast.187, bf16[256,2048]{1,0:T(8,128)(2,1)} %copy-done.13, bf16[256,2048]{1,0:T(8,128)(2,1)} %copy-done.17, ...), custom_call_target="tpu_custom_call", output_to_operand_aliasing={{0}: (11, {})} | custom-call | tf_op jit(solution)/shard_map/conv_forward/pallas_call | solution.py:421
  169.7 14.0 %scan_forward.2 = (bf16[2048,1024]{1,0:T(8,128)(2,1)}, f32[8,16,1024]{2,1,0:T(8,128)}) custom-call(s32[4]{0:T(128)} %copy-done.26, s32[2]{0:T(128)} %bitcast.188, f32[1280,128]{1,0:T(8,128)} %convert_add_fusion.5.refs_2_, bf16[1024,1024]{1,0:T(8,128)(2,1)} %get-tuple-element.130.refs_3_.refs_6_, bf16[128,1024]{1,0:T(8,128)(2,1)} %slice.222.refs_4_.refs_6_, ...), custom_call_target="tpu_custom_call" | custom-call | tf_op jit(solution)/shard_map/scan_forward/pallas_call | solution.py:142
  184.6 14.0 %scan_forward.3 = (bf16[2048,1024]{1,0:T(8,128)(2,1)}, f32[8,16,1024]{2,1,0:T(8,128)}) custom-call(s32[4]{0:T(128)} %copy-done.26, s32[2]{0:T(128)} %bitcast.189, f32[1280,128]{1,0:T(8,128)} %convert_add_fusion.6.refs_2_, bf16[1024,1024]{1,0:T(8,128)(2,1)} %get-tuple-element.128.refs_3_.refs_6_, ...), custom_call_target="tpu_custom_call", output_to_operand_aliasing={{0}: (8, {})} | custom-call | tf_op jit(solution)/shard_map/scan_forward/pallas_call | solution.py:142
  198.7 15.9 %fusion.1 = (bf16[2048,1024]{1,0:T(8,128)(2,1)S(1)}, f32[2048,1024]{1,0:T(8,128)}) fusion(bf16[2048,1024]{1,0:T(8,128)(2,1)} %get-tuple-element.134, bf16[2048,2048]{1,0:T(8,128)(2,1)} %get-tuple-element.133, bf16[2048,1024]{1,0:T(8,128)(2,1)} %all-gather.5.cloned.1.call-done), kind=kOutput, calls=%fused_computation.4 | convolution fusion | flops 8604614656 | bytes 29360128 | tf_op jit(solution)/shard_map/dot_general | solution.py:585
  223.4 11.0 %fusion.36 = bf16[1024,2048]{1,0:T(8,128)(2,1)} fusion(bf16[2048,1024]{1,0:T(8,128)(2,1)S(1)} %get-tuple-element.138, bf16[2048,2048]{1,0:T(8,128)(2,1)S(1)} %bitcast.165), kind=kOutput, calls=%fused_computation.118 | convolution fusion | flops 8589934592 | bytes 16777216 | tf_op jit(solution)/shard_map/dot_general | solution.py:585
  234.6 22.4 %all-gather.7.cloned.1.call-done = bf16[1024,2048]{1,0:T(8,128)(2,1)} async-done(((bf16[128,2048]{1,0:T(8,128)(2,1)}), bf16[1024,2048]{1,0:T(8,128)(2,1)}) %all-gather.7.cloned.1.call-update) | async-done | bytes 4194320 | tf_op jit(solution)/shard_map/all_gather | solution.py:627
  272.7 19.9 %multiply_convert_fusion = (bf16[2048,1024]{1,0:T(8,128)(2,1)}, bf16[2048,1024]{1,0:T(8,128)(2,1)}) fusion(f32[2048,1024]{1,0:T(8,128)} %get-tuple-element.265, bf16[2048,1024]{1,0:T(8,128)(2,1)S(1)} %copy-done.11, bf16[2048,2048]{1,0:T(8,128)(2,1)} %bitcast.166, bf16[1024,2048]{1,0:T(8,128)(2,1)} %all-gather.7.cloned.1.call-done), kind=kOutput, calls=%fused_computation.11 | convolution fusion | flops 8619294720 | bytes 33554432 | tf_op jit(solution)/shard_map/dot_general | solution.py:585
  292.6 12.4 %fusion.37 = bf16[2048,1024]{1,0:T(8,128)(2,1)} fusion(bf16[2048,2048]{1,0:T(8,128)(2,1)S(1)} %bitcast.164, bf16[2048,1024]{1,0:T(8,128)(2,1)} %get-tuple-element.158), kind=kOutput, calls=%fused_computation.119 | convolution fusion | flops 8589934592 | bytes 16777216 | tf_op jit(solution)/shard_map/dot_general | solution.py:585
  314.3 35.6 %scan_backward.3 = (f32[1280,128]{1,0:T(8,128)}, bf16[1024,1024]{1,0:T(8,128)(2,1)}, f32[128,1024]{1,0:T(8,128)}, f32[1,1024]{1,0:T(1,128)}, f32[16,1024]{1,0:T(8,128)}, /*index=5*/f32[1,1024]{1,0:T(1,128)}) custom-call(s32[4]{0:T(128)} %copy-done.26, s32[2]{0:T(128)} %bitcast.190, f32[1280,128]{1,0:T(8,128)} %convert_add_fusion.5.refs_2_, ...), custom_call_target="tpu_custom_call" | custom-call | tf_op jit(solution)/shard_map/scan_backward/pallas_call | solution.py:322
  366.4 35.1 %scan_backward.2 = (f32[1280,128]{1,0:T(8,128)}, bf16[1024,1024]{1,0:T(8,128)(2,1)}, f32[128,1024]{1,0:T(8,128)}, f32[1,1024]{1,0:T(1,128)}, f32[16,1024]{1,0:T(8,128)}, /*index=5*/f32[1,1024]{1,0:T(1,128)}) custom-call(s32[4]{0:T(128)} %copy-done.26, s32[2]{0:T(128)} %bitcast.191, f32[1280,128]{1,0:T(8,128)} %convert_add_fusion.6.refs_2_, ...), custom_call_target="tpu_custom_call" | custom-call | tf_op jit(solution)/shard_map/scan_backward/pallas_call | solution.py:322
  407.5 11.6 %conv_backward.2 = (bf16[2048,1024]{1,0:T(8,128)(2,1)}, f32[160,1024]{1,0:T(8,128)}, f32[1,1024]{1,0:T(1,128)}, f32[4,1024]{1,0:T(4,128)}) custom-call(s32[4]{0:T(128)} %copy-done.26, s32[2]{0:T(128)} %bitcast.192, f32[1280,128]{1,0:T(8,128)} %convert_add_fusion.4.refs_2_, bf16[1024,1024]{1,0:T(8,128)(2,1)} %get-tuple-element.154.refs_3_, ...), custom_call_target="tpu_custom_call" | custom-call | tf_op jit(solution)/shard_map/conv_backward/pallas_call | solution.py:504
  420.7 15.5 %fusion.38 = f32[2048,2048]{1,0:T(8,128)} fusion(bf16[2048,1024]{1,0:T(8,128)(2,1)} %get-tuple-element.158, bf16[2048,1024]{1,0:T(8,128)(2,1)} %all-gather.5.cloned.1.call-done), kind=kOutput, calls=%fused_computation.120 | convolution fusion | flops 8589934592 | bytes 25165824 | tf_op jit(solution)/shard_map/dot_general | solution.py:585
  437.1 11.5 %conv_backward.3 = (bf16[2048,1024]{1,0:T(8,128)(2,1)}, f32[160,1024]{1,0:T(8,128)}, f32[1,1024]{1,0:T(1,128)}, f32[4,1024]{1,0:T(4,128)}) custom-call(s32[4]{0:T(128)} %copy-done.26, s32[2]{0:T(128)} %bitcast.193, f32[1280,128]{1,0:T(8,128)} %convert_add_fusion.3.refs_2_, ...), custom_call_target="tpu_custom_call", output_to_operand_aliasing={{0}: (10, {})} | custom-call | tf_op jit(solution)/shard_map/conv_backward/pallas_call | solution.py:504
  451.3 14.0 %fusion.39 = bf16[2048,1024]{1,0:T(8,128)(2,1)} fusion(bf16[2048,2048]{1,0:T(8,128)(2,1)} %get-tuple-element.133, bf16[2048,1024]{1,0:T(8,128)(2,1)} %get-tuple-element.179), kind=kOutput, calls=%fused_computation.121 | convolution fusion | flops 8589934592 | bytes 16777216 | tf_op jit(solution)/shard_map/dot_general | solution.py:585
  465.3 12.5 %fusion.40 = f32[2048,2048]{1,0:T(8,128)S(1)} fusion(bf16[2048,1024]{1,0:T(8,128)(2,1)} %get-tuple-element.179, bf16[2048,1024]{1,0:T(8,128)(2,1)} %bitcast.167), kind=kOutput, calls=%fused_computation.122 | convolution fusion | flops 8589934592 | bytes 25165824 | tf_op jit(solution)/shard_map/dot_general | solution.py:585
  490.8 31.1 %collective-permute-start.23 = (bf16[4,311,128]{2,1,0:T(8,128)(2,1)S(1)}, bf16[4,311,128]{2,1,0:T(8,128)(2,1)S(1)}, u32[]{:S(2)}, u32[]{:S(2)}) collective-permute-start(bf16[4,311,128]{2,1,0:T(8,128)(2,1)S(1)} %fusion.23), channel_id=1, source_target_pairs={{0,4},{4,0},{8,12},{12,8},{16,20},{20,16},{24,28},{28,24},{1,5},{5... | collective-permute-start | bytes 955400 | tf_op jit(solution)/shard_map/ppermute | solution.py:578
  530.0 54.5 %collective-permute-start.24 = (bf16[2,311,128]{2,1,0:T(8,128)(2,1)S(1)}, bf16[2,311,128]{2,1,0:T(8,128)(2,1)S(1)}, u32[]{:S(2)}, u32[]{:S(2)}) collective-permute-start(bf16[2,311,128]{2,1,0:T(8,128)(2,1)S(1)} %fusion.26), channel_id=1, source_target_pairs={{0,8},{4,12},{8,0},{12,4},{16,24},{20,28},{24,16},{28,20},{1,9},{5... | collective-permute-start | bytes 477704 | tf_op jit(solution)/shard_map/ppermute | solution.py:578
  584.5 14.2 %collective-permute-done.24 = bf16[2,311,128]{2,1,0:T(8,128)(2,1)S(1)} collective-permute-done((bf16[2,311,128]{2,1,0:T(8,128)(2,1)S(1)}, bf16[2,311,128]{2,1,0:T(8,128)(2,1)S(1)}, u32[]{:S(2)}, u32[]{:S(2)}) %collective-permute-start.24) | collective-permute-done | bytes 159264 | tf_op jit(solution)/shard_map/ppermute | solution.py:578
  625.4 25.3 %reduce-scatter.6.cloned.1.call-done = bf16[256,1024]{1,0:T(8,128)(2,1)} async-done(((bf16[2048,1024]{1,0:T(8,128)(2,1)}), bf16[256,1024]{1,0:T(8,128)(2,1)}) %reduce-scatter.6.cloned.1.call-update) | async-done | bytes 524304 | tf_op jit(solution)/shard_map/reduce_scatter | solution.py:709
  (282 shorter events, 189.7 us)
Async XLA Ops:
  7.3 15.3 %collective-permute-start.6 = (bf16[64]{0:T(256)(128)(2,1)}, bf16[64]{0:T(256)(128)(2,1)S(1)}, u32[]{:S(2)}, u32[]{:S(2)}) collective-permute-start(bf16[64]{0:T(256)(128)(2,1)} %param.16), channel_id=1, source_target_pairs={{0,2},{1,3},{2,0},{3,1},{4,6},{5,7},{6,4},{7,5},{8,10},{9,11},{10,... | collective-permute-start | bytes 392 | tf_op jit(solution)/shard_map/ppermute | solution.py:535
  17.4 93.0 %all-gather.9.cloned.1.call-start = ((), (), s32[]{:S(2)}) async-start(), calls=%async_computation.12 | async-start | bytes 5455872 | tf_op jit(solution)/shard_map/all_gather | solution.py:620
  27.8 170.9 %all-gather.5.cloned.1.call-start = ((), (), s32[]{:S(2)}) async-start(), calls=%async_computation.7 | async-start | bytes 4718592 | tf_op jit(solution)/shard_map/all_gather | solution.py:626
  28.1 26.1 %collective-permute-start.3 = (bf16[256,2048]{1,0:T(8,128)(2,1)S(1)}, bf16[256,2048]{1,0:T(8,128)(2,1)S(1)}, u32[]{:S(2)}, u32[]{:S(2)}) collective-permute-start(bf16[256,2048]{1,0:T(8,128)(2,1)S(1)} %get-tuple-element.121.refs_2_), channel_id=1, source_target_pairs={{0,2},{1,3},{2,0},{3,1},{4,6},{5,7},{6,4},{7,5},{8,10},{9,11},{10,... | collective-permute-start | bytes 3145736 | tf_op jit(solution)/shard_map/ppermute | solution.py:535
  29.8 46.2 %collective-permute-start = (bf16[256,2048]{1,0:T(8,128)(2,1)S(1)}, bf16[256,2048]{1,0:T(8,128)(2,1)S(1)}, u32[]{:S(2)}, u32[]{:S(2)}) collective-permute-start(bf16[256,2048]{1,0:T(8,128)(2,1)S(1)} %get-tuple-element.111.refs_2_), channel_id=1, source_target_pairs={{0,2},{1,3},{2,0},{3,1},{4,6},{5,7},{6,4},{7,5},{8,10},{9,11},{10,... | collective-permute-start | bytes 3145736 | tf_op jit(solution)/shard_map/ppermute | solution.py:535
  30.2 45.8 %collective-permute-start.4 = (bf16[256,2048]{1,0:T(8,128)(2,1)S(1)}, bf16[256,2048]{1,0:T(8,128)(2,1)S(1)}, u32[]{:S(2)}, u32[]{:S(2)}) collective-permute-start(bf16[256,2048]{1,0:T(8,128)(2,1)S(1)} %get-tuple-element.121.refs_2_), channel_id=1, source_target_pairs={{0,1},{1,0},{2,3},{3,2},{4,5},{5,4},{6,7},{7,6},{8,9},{9,8},{10,11... | collective-permute-start | bytes 3145736 | tf_op jit(solution)/shard_map/ppermute | solution.py:535
  30.2 45.8 %collective-permute-start.1 = (bf16[256,2048]{1,0:T(8,128)(2,1)S(1)}, bf16[256,2048]{1,0:T(8,128)(2,1)S(1)}, u32[]{:S(2)}, u32[]{:S(2)}) collective-permute-start(bf16[256,2048]{1,0:T(8,128)(2,1)S(1)} %get-tuple-element.111.refs_2_), channel_id=1, source_target_pairs={{0,1},{1,0},{2,3},{3,2},{4,5},{5,4},{6,7},{7,6},{8,9},{9,8},{10,11... | collective-permute-start | bytes 3145736 | tf_op jit(solution)/shard_map/ppermute | solution.py:535
  54.2 21.8 %collective-permute-start.5 = (bf16[256,2048]{1,0:T(8,128)(2,1)S(1)}, bf16[256,2048]{1,0:T(8,128)(2,1)S(1)}, u32[]{:S(2)}, u32[]{:S(2)}) collective-permute-start(bf16[256,2048]{1,0:T(8,128)(2,1)S(1)} %collective-permute-done.3.refs_3_), channel_id=1, source_target_pairs={{0,1},{1,0},{2,3},{3,2},{4,5},{5,4},{6,7},{7,6},{8,9},{9,8},{10,11... | collective-permute-start | bytes 3145736 | tf_op jit(solution)/shard_map/ppermute | solution.py:535
  93.3 163.8 %all-gather.7.cloned.1.call-start = ((), (), s32[]{:S(2)}) async-start(), calls=%async_computation.8 | async-start | bytes 4718592 | tf_op jit(solution)/shard_map/all_gather | solution.py:627
  95.8 47.5 %collective-permute-start.9 = (bf16[2,256,2048]{2,1,0:T(8,128)(2,1)S(1)}, bf16[2,256,2048]{2,1,0:T(8,128)(2,1)}, u32[]{:S(2)}, u32[]{:S(2)}) collective-permute-start(bf16[2,256,2048]{2,1,0:T(8,128)(2,1)S(1)} %fusion.15), channel_id=1, source_target_pairs={{0,2},{1,3},{2,0},{3,1},{4,6},{5,7},{6,4},{7,5},{8,10},{9,11},{10,... | collective-permute-start | bytes 6291464 | tf_op jit(solution)/shard_map/ppermute | solution.py:535
  156.3 210.1 %reduce-scatter.4.cloned.1.call-start = ((), (), s32[]{:S(2)}) async-start(), calls=%async_computation.9 | async-start | bytes 4718592 | tf_op jit(solution)/shard_map/reduce_scatter | solution.py:679
  158.9 55.8 %collective-permute-start.13 = (bf16[2,256,2048]{2,1,0:T(8,128)(2,1)S(1)}, bf16[2,256,2048]{2,1,0:T(8,128)(2,1)}, u32[]{:S(2)}, u32[]{:S(2)}) collective-permute-start(bf16[2,256,2048]{2,1,0:T(8,128)(2,1)S(1)} %fusion.15), channel_id=1, source_target_pairs={{0,1},{1,0},{2,3},{3,2},{4,5},{5,4},{6,7},{7,6},{8,9},{9,8},{10,11... | collective-permute-start | bytes 6291464 | tf_op jit(solution)/shard_map/ppermute | solution.py:535
  159.1 55.5 %collective-permute-start.14 = (bf16[2,256,2048]{2,1,0:T(8,128)(2,1)}, bf16[2,256,2048]{2,1,0:T(8,128)(2,1)}, u32[]{:S(2)}, u32[]{:S(2)}) collective-permute-start(bf16[2,256,2048]{2,1,0:T(8,128)(2,1)} %collective-permute-done.9), channel_id=1, source_target_pairs={{0,1},{1,0},{2,3},{3,2},{4,5},{5,4},{6,7},{7,6},{8,9},{9,8},{10,11... | collective-permute-start | bytes 6291464 | tf_op jit(solution)/shard_map/ppermute | solution.py:535
  160.7 23.0 %collective-permute-start.11 = (bf16[1280,128]{1,0:T(8,128)(2,1)S(1)}, bf16[1280,128]{1,0:T(8,128)(2,1)S(1)}, u32[]{:S(2)}, u32[]{:S(2)}) collective-permute-start(bf16[1280,128]{1,0:T(8,128)(2,1)S(1)} %add_convert_fusion.5), channel_id=1, source_target_pairs={{0,2},{1,3},{2,0},{3,1},{4,6},{5,7},{6,4},{7,5},{8,10},{9,11},{10,... | collective-permute-start | bytes 983048 | tf_op jit(solution)/shard_map/ppermute | solution.py:535
  234.4 378.7 %reduce-scatter.8.cloned.1.call-start = ((), (), s32[]{:S(2)}) async-start(), calls=%async_computation.11 | async-start | bytes 4718592 | tf_op jit(solution)/shard_map/reduce_scatter | solution.py:680
  312.6 48.7 %collective-permute-start.16 = (bf16[512,2048]{1,0:T(8,128)(2,1)S(1)}, bf16[512,2048]{1,0:T(8,128)(2,1)}, u32[]{:S(2)}, u32[]{:S(2)}) collective-permute-start(bf16[512,2048]{1,0:T(8,128)(2,1)S(1)} %slice.190), channel_id=1, source_target_pairs={{0,2},{1,3},{2,0},{3,1},{4,6},{5,7},{6,4},{7,5},{8,10},{9,11},{10,... | collective-permute-start | bytes 6291464 | tf_op jit(solution)/shard_map/ppermute | solution.py:535
  314.2 336.5 %reduce-scatter.6.cloned.1.call-start = ((), (), s32[]{:S(2)}) async-start(), calls=%async_computation.10 | async-start | bytes 4718592 | tf_op jit(solution)/shard_map/reduce_scatter | solution.py:709
  353.4 53.0 %collective-permute-start.19 = (bf16[1280,128]{1,0:T(8,128)(2,1)S(1)}, bf16[1280,128]{1,0:T(8,128)(2,1)S(1)}, u32[]{:S(2)}, u32[]{:S(2)}) collective-permute-start(bf16[1280,128]{1,0:T(8,128)(2,1)S(1)} %add_convert_fusion.3), channel_id=1, source_target_pairs={{0,2},{1,3},{2,0},{3,1},{4,6},{5,7},{6,4},{7,5},{8,10},{9,11},{10,... | collective-permute-start | bytes 983048 | tf_op jit(solution)/shard_map/ppermute | solution.py:535
  401.6 17.5 %collective-permute-start.17 = (f32[1280,128]{1,0:T(8,128)}, f32[1280,128]{1,0:T(8,128)S(1)}, u32[]{:S(2)}, u32[]{:S(2)}) collective-permute-start(f32[1280,128]{1,0:T(8,128)} %get-tuple-element.149), channel_id=1, source_target_pairs={{0,1},{1,0},{2,3},{3,2},{4,5},{5,4},{6,7},{7,6},{8,9},{9,8},{10,11... | collective-permute-start | bytes 1966088 | tf_op jit(solution)/shard_map/ppermute | solution.py:535
  419.2 17.0 %collective-permute-start.20 = (bf16[1280,128]{1,0:T(8,128)(2,1)S(1)}, bf16[1280,128]{1,0:T(8,128)(2,1)S(1)}, u32[]{:S(2)}, u32[]{:S(2)}) collective-permute-start(bf16[1280,128]{1,0:T(8,128)(2,1)S(1)} %add_convert_fusion.4), channel_id=1, source_target_pairs={{0,2},{1,3},{2,0},{3,1},{4,6},{5,7},{6,4},{7,5},{8,10},{9,11},{10,... | collective-permute-start | bytes 983048 | tf_op jit(solution)/shard_map/ppermute | solution.py:535
  489.5 32.4 %collective-permute-start.21 = (bf16[1024,2048]{1,0:T(8,128)(2,1)}, bf16[1024,2048]{1,0:T(8,128)(2,1)}, u32[]{:S(2)}, u32[]{:S(2)}) collective-permute-start(bf16[1024,2048]{1,0:T(8,128)(2,1)} %slice.228), channel_id=1, source_target_pairs={{0,1},{1,0},{2,3},{3,2},{4,5},{5,4},{6,7},{7,6},{8,9},{9,8},{10,11... | collective-permute-start | bytes 12582920 | tf_op jit(solution)/shard_map/ppermute | solution.py:535
  490.8 39.1 %collective-permute-start.23 = (bf16[4,311,128]{2,1,0:T(8,128)(2,1)S(1)}, bf16[4,311,128]{2,1,0:T(8,128)(2,1)S(1)}, u32[]{:S(2)}, u32[]{:S(2)}) collective-permute-start(bf16[4,311,128]{2,1,0:T(8,128)(2,1)S(1)} %fusion.23), channel_id=1, source_target_pairs={{0,4},{4,0},{8,12},{12,8},{16,20},{20,16},{24,28},{28,24},{1,5},{5... | collective-permute-start | bytes 955400 | tf_op jit(solution)/shard_map/ppermute | solution.py:578
  528.8 87.9 %collective-permute-start.22 = (bf16[512,2048]{1,0:T(8,128)(2,1)}, bf16[512,2048]{1,0:T(8,128)(2,1)}, u32[]{:S(2)}, u32[]{:S(2)}) collective-permute-start(bf16[512,2048]{1,0:T(8,128)(2,1)} %slice.230), channel_id=1, source_target_pairs={{0,2},{1,3},{2,0},{3,1},{4,6},{5,7},{6,4},{7,5},{8,10},{9,11},{10,... | collective-permute-start | bytes 6291464 | tf_op jit(solution)/shard_map/ppermute | solution.py:535
  530.0 68.7 %collective-permute-start.24 = (bf16[2,311,128]{2,1,0:T(8,128)(2,1)S(1)}, bf16[2,311,128]{2,1,0:T(8,128)(2,1)S(1)}, u32[]{:S(2)}, u32[]{:S(2)}) collective-permute-start(bf16[2,311,128]{2,1,0:T(8,128)(2,1)S(1)} %fusion.26), channel_id=1, source_target_pairs={{0,8},{4,12},{8,0},{12,4},{16,24},{20,28},{24,16},{28,20},{1,9},{5... | collective-permute-start | bytes 477704 | tf_op jit(solution)/shard_map/ppermute | solution.py:578
  (63 other events, 1252.3 us)
Sparse Core Ops, SparseCore 0:
  27.9 82.3 all-gather.8
  112.4 71.1 all-gather.4
  185.7 71.3 all-gather.6
  260.6 87.9 reduce-scatter.3
  352.0 87.9 reduce-scatter.7
  465.4 185.2 reduce-scatter.5
where the time goes:
time: 674 us; the launch traced here: 680 us
  waiting for transfers between devices  157 us (23%)
  Pallas kernels  147 us (22%)
  starting transfers between devices  122 us (18%)
  matrix products  117 us (17%)
  other arithmetic  61.6 us (9%)
  local copies, waits for them, and re-layouts  40.5 us (6%)
  between operations  23.4 us (3%)
  blocking collectives  11.9 us (2%)
    dot_general x9, matrix products, dot(): lax.dot_general(left, right, (dims, ((), ())), preferred_element_type=kind)  117 us
    ppermute x3, starting transfers between devices, sum_to_owner(): other = lax.ppermute(given, 'dp', [(i, i ^ step) for i in range(ranks)])  95.7 us
    ppermute x23, waiting for transfers between devices, partner(): return lax.ppermute(value, 'seq', [(i, i ^ step) for i in range(peers)])  74.1 us
    pallas_call x2, Pallas kernels, scan_backward(): pl.pallas_call(lambda *refs: scan_backward_kernel(*refs, width=width, mic...  70.7 us
    pallas_call x2, Pallas kernels, scan_forward(): pl.pallas_call(lambda *refs: scan_forward_kernel(*refs, width=width, micr...  28.1 us
    pallas_call x2, Pallas kernels, conv_forward(): pl.pallas_call(lambda *refs: conv_forward_kernel(*refs, peers=peers, micr...  25.5 us
    reduce_scatter x1, waiting for transfers between devices, body(): gwb = lax.psum_scatter(gwb, 'dp', scatter_dimension=0, tiled=True)  25.3 us
    pallas_call x2, Pallas kernels, conv_backward(): pl.pallas_call(lambda *refs: conv_backward_kernel(*refs, micro=micro), gr...  23.1 us
  transfers between devices with their start and end apart: 35, of which 16 were waited for; matrix products, arithmetic and copies ran while one was open for 29% of the time, Pallas kernels for 22%

commit v1 on v0

--- a/solution.py
+++ b/solution.py
@@ -392,10 +392,7 @@
 
     @pl.when(live)
     def _():
-        groups = wb_ref.shape[0]
-        deep = normed_ref.shape[1] // groups
-        branch = sum(jnp.dot(normed_ref[:, d * deep:(d + 1) * deep], wb_ref[d, 0:deep, :], preferred_element_type=F32)
-                     for d in range(groups)).astype(BF16)
+        branch = jnp.dot(normed_ref[...], wb_ref[...], preferred_element_type=F32).astype(BF16)
         branch_ref[...] = branch
         pad[8:8 + length, :] = branch.astype(F32)
         pre = cb_ref[...] + sum(cw_ref[k:k + 1, :] * pad[5 + k:5 + k + length, :] for k in range(KCONV))
@@ -414,7 +411,7 @@
 def conv_forward(order, lengths, pieces, gain, wb, cw, cb, xw, rank, micro, micros, held):
     peers = len(pieces)
     tokens, width = pieces[0].shape
-    inner = wb.shape[2]
+    inner = wb.shape[1]
     cols = xw.shape[0]
     rows = tokens // CHUNK * (CHUNK + cols - rank)
     first = held is None
@@ -625,6 +622,7 @@
     late, pieces = lax.optimization_barrier((in_weight[:, inner * peers:], pieces))
     wg = lax.all_gather(mine(late), "dp", axis=0, tiled=True)
     wo = lax.all_gather(out_weight, "dp", axis=0, tiled=True)
+    wb = first[:, :peers * rows].reshape(width, inner)
     small = first[:, peers * rows:].reshape(groups, packed, share)
     at = states + KCONV + 3
     gain = small[:, at:at + gain_rows].reshape(1, width).astype(F32)
@@ -647,7 +645,7 @@
         grads = grads + [partner(part, step) for part in grads]
     convs, normed = [], None
     for m in range(micros):
-        normed, branch, x, proj = conv_forward(order, held, pieces[m], gain, first, cw, cb, xw, rank, m, micros, normed)
+        normed, branch, x, proj = conv_forward(order, held, pieces[m], gain, wb, cw, cb, xw, rank, m, micros, normed)
         proj = (proj + partner(proj, 1)).astype(BF16)
         if m + 1 < micros:
             proj, pieces[m + 1], grads = lax.optimization_barrier((proj, pieces[m + 1], grads))
@@ -708,7 +706,6 @@
     gwb, totals, mixed = lax.optimization_barrier((gwb, totals, mixed))
     gwb = lax.psum_scatter(gwb, "dp", scatter_dimension=0, tiled=True)
     gsmall = sum_to_owner(jnp.concatenate(totals, axis=0))
-    wb = first[:, :peers * rows].reshape(width, inner)
     w = (early + dot(mixed, wb, ((1,), (1,)))).astype(BF16)
     w = finish_piece((w[:half].astype(F32) + partner(w[half:], 1).astype(F32)).astype(BF16)).reshape(micros, piece, width)
     w, gwb, gsmall, gwg = lax.optimization_barrier((w, gwb, gsmall, gwg))

time: 674 us -> 688 us (1.021)
  Pallas kernels: 147 us -> 182 us
  waiting for transfers between devices: 157 us -> 128 us
  other arithmetic: 61.6 us -> 69.8 us
  starting transfers between devices: 122 us -> 115 us
    pallas_call x2, Pallas kernels: 70.7 us -> 97.8 us  [scan_backward(): pl.pallas_call(lambda *refs: scan_backward_kernel(*refs, width=width, mic...]
    ppermute x23, waiting for transfers between devices: 74.1 us -> 59.6 us  [partner(): return lax.ppermute(value, 'seq', [(i, i ^ step) for i in range(peers)])]
    ppermute x3, waiting for transfers between devices: 16 us -> 4.4 us  [sum_to_owner(): other = lax.ppermute(given, 'dp', [(i, i ^ step) for i in range(ranks)])]
  transfers between devices with their start and end apart: 35 -> 35, of which waited for: 16 -> 13; matrix products, arithmetic and copies ran while one was open for 29% -> 30% of each run, Pallas kernels for 22% -> 26%
where the time goes in v1:
time: 688 us; the launch traced here: 690 us
  Pallas kernels  182 us (26%)
  waiting for transfers between devices  128 us (19%)
  matrix products  116 us (17%)
  starting transfers between devices  115 us (17%)
  other arithmetic  69.8 us (10%)
  local copies, waits for them, and re-layouts  43.5 us (6%)
  between operations  23.4 us (3%)
  blocking collectives  11.9 us (2%)
    dot_general x9, matrix products, dot(): lax.dot_general(left, right, (dims, ((), ())), preferred_element_type=kind)  116 us
    pallas_call x2, Pallas kernels, scan_backward(): pl.pallas_call(lambda *refs: scan_backward_kernel(*refs, width=width, mic...  97.8 us
    ppermute x3, starting transfers between devices, sum_to_owner(): other = lax.ppermute(given, 'dp', [(i, i ^ step) for i in range(ranks)])  89 us
    ppermute x23, waiting for transfers between devices, partner(): return lax.ppermute(value, 'seq', [(i, i ^ step) for i in range(peers)])  59.6 us
    pallas_call x2, Pallas kernels, scan_forward(): pl.pallas_call(lambda *refs: scan_forward_kernel(*refs, width=width, micr...  34.8 us
    reduce_scatter x1, waiting for transfers between devices, body(): gwb = lax.psum_scatter(gwb, 'dp', scatter_dimension=0, tiled=True)  29.8 us
    pallas_call x2, Pallas kernels, conv_forward(): pl.pallas_call(lambda *refs: conv_forward_kernel(*refs, peers=peers, micr...  25.2 us
    pallas_call x2, Pallas kernels, conv_backward(): pl.pallas_call(lambda *refs: conv_backward_kernel(*refs, micro=micro), gr...  24.7 us
  transfers between devices with their start and end apart: 35, of which 13 were waited for; matrix products, arithmetic and copies ran while one was open for 30% of the time, Pallas kernels for 26%

profile of v1, /device:TPU:0, one launch (start us, length us, event | category | flops | bytes accessed | tf_op | source)
XLA Modules:
  0.0 690.1 jit_solution(15881998343475277151)
XLA Ops:
  30.7 23.5 %collective-permute-done.refs_3_ = bf16[256,2048]{1,0:T(8,128)(2,1)S(1)} collective-permute-done((bf16[256,2048]{1,0:T(8,128)(2,1)S(1)}, bf16[256,2048]{1,0:T(8,128)(2,1)S(1)}, u32[]{:S(2)}, u32[]{:S(2)}) %collective-permute-start) | collective-permute-done | bytes 1048608 | tf_op jit(solution)/shard_map/ppermute | solution.py:532
  54.2 21.8 %collective-permute-done.3.refs_3_ = bf16[256,2048]{1,0:T(8,128)(2,1)S(1)} collective-permute-done((bf16[256,2048]{1,0:T(8,128)(2,1)S(1)}, bf16[256,2048]{1,0:T(8,128)(2,1)S(1)}, u32[]{:S(2)}, u32[]{:S(2)}) %collective-permute-start.3) | collective-permute-done | bytes 1048608 | tf_op jit(solution)/shard_map/ppermute | solution.py:532
  81.5 11.9 %all_to_all.45 = bf16[4,64,1024]{2,1,0:T(8,128)(2,1)} all-to-all(bf16[4,64,1024]{2,1,0:T(8,128)(2,1)S(1)} %all_to_all.33), channel_id=1, replica_groups=mesh['dp'=8,'seq'=4] {'seq'}, dimensions={0} | all-to-all | bytes 1048576 | tf_op jit(solution)/shard_map/all_to_all | solution.py:614
  96.5 13.8 %all-gather.9.cloned.1.call-done = bf16[2368,1024]{1,0:T(8,128)(2,1)} async-done(((bf16[296,1024]{1,0:T(8,128)(2,1)}), bf16[2368,1024]{1,0:T(8,128)(2,1)}) %all-gather.9.cloned.1.call-update) | async-done | bytes 4849680 | tf_op jit(solution)/shard_map/all_gather | solution.py:617
  126.9 13.4 %conv_forward.2 = (bf16[2048,2048]{1,0:T(8,128)(2,1)}, bf16[1024,1024]{1,0:T(8,128)(2,1)}, bf16[1024,1024]{1,0:T(8,128)(2,1)}, f32[1280,128]{1,0:T(8,128)}) custom-call(s32[4]{0:T(128)} %copy-done.25, s32[2]{0:T(128)} %bitcast.186, bf16[256,2048]{1,0:T(8,128)(2,1)} %copy-done.11, bf16[256,2048]{1,0:T(8,128)(2,1)} %copy-done.13, ...), custom_call_target="tpu_custom_call" | custom-call | tf_op jit(solution)/shard_map/conv_forward/pallas_call | solution.py:418
  143.8 11.8 %conv_forward.3 = (bf16[2048,2048]{1,0:T(8,128)(2,1)}, bf16[1024,1024]{1,0:T(8,128)(2,1)}, bf16[1024,1024]{1,0:T(8,128)(2,1)}, f32[1280,128]{1,0:T(8,128)}) custom-call(s32[4]{0:T(128)} %copy-done.25, s32[2]{0:T(128)} %bitcast.187, bf16[256,2048]{1,0:T(8,128)(2,1)} %copy-done.12, bf16[256,2048]{1,0:T(8,128)(2,1)} %copy-done.16, ...), custom_call_target="tpu_custom_call", output_to_operand_aliasing={{0}: (11, {})} | custom-call | tf_op jit(solution)/shard_map/conv_forward/pallas_call | solution.py:418
  169.5 20.7 %scan_forward.2 = (bf16[2048,1024]{1,0:T(8,128)(2,1)}, f32[8,16,1024]{2,1,0:T(8,128)}) custom-call(s32[4]{0:T(128)} %copy-done.25, s32[2]{0:T(128)} %bitcast.188, f32[1280,128]{1,0:T(8,128)} %convert_add_fusion.5.refs_2_, bf16[1024,1024]{1,0:T(8,128)(2,1)} %get-tuple-element.130.refs_3_.refs_6_, bf16[128,1024]{1,0:T(8,128)(2,1)} %slice.223.refs_4_.refs_6_, ...), custom_call_target="tpu_custom_call" | custom-call | tf_op jit(solution)/shard_map/scan_forward/pallas_call | solution.py:142
  191.1 14.1 %scan_forward.3 = (bf16[2048,1024]{1,0:T(8,128)(2,1)}, f32[8,16,1024]{2,1,0:T(8,128)}) custom-call(s32[4]{0:T(128)} %copy-done.25, s32[2]{0:T(128)} %bitcast.189, f32[1280,128]{1,0:T(8,128)} %convert_add_fusion.6.refs_2_, bf16[1024,1024]{1,0:T(8,128)(2,1)} %get-tuple-element.128.refs_3_.refs_6_, ...), custom_call_target="tpu_custom_call", output_to_operand_aliasing={{0}: (8, {})} | custom-call | tf_op jit(solution)/shard_map/scan_forward/pallas_call | solution.py:142
  205.2 15.9 %fusion.1 = (bf16[2048,1024]{1,0:T(8,128)(2,1)S(1)}, f32[2048,1024]{1,0:T(8,128)}) fusion(bf16[2048,1024]{1,0:T(8,128)(2,1)} %get-tuple-element.134, bf16[2048,2048]{1,0:T(8,128)(2,1)} %get-tuple-element.133, bf16[2048,1024]{1,0:T(8,128)(2,1)} %all-gather.5.cloned.1.call-done), kind=kOutput, calls=%fused_computation.4 | convolution fusion | flops 8604614656 | bytes 29360128 | tf_op jit(solution)/shard_map/dot_general | solution.py:582
  241.2 15.9 %all-gather.7.cloned.1.call-done = bf16[1024,2048]{1,0:T(8,128)(2,1)} async-done(((bf16[128,2048]{1,0:T(8,128)(2,1)}), bf16[1024,2048]{1,0:T(8,128)(2,1)}) %all-gather.7.cloned.1.call-update) | async-done | bytes 4194320 | tf_op jit(solution)/shard_map/all_gather | solution.py:624
  257.1 20.9 %multiply_convert_fusion = (bf16[2048,1024]{1,0:T(8,128)(2,1)}, bf16[2048,1024]{1,0:T(8,128)(2,1)S(1)}) fusion(f32[2048,1024]{1,0:T(8,128)} %get-tuple-element.265, bf16[2048,1024]{1,0:T(8,128)(2,1)} %get-tuple-element.134, bf16[2048,2048]{1,0:T(8,128)(2,1)} %bitcast.162, bf16[1024,2048]{1,0:T(8,128)(2,1)} %all-gather.7.cloned.1.call-done), kind=kOutput, calls=%fused_computation.11 | convolution fusion | flops 8619294720 | bytes 33554432 | tf_op jit(solution)/shard_map/dot_general | solution.py:582
  290.2 11.2 %fusion.37 = bf16[2048,1024]{1,0:T(8,128)(2,1)} fusion(bf16[2048,2048]{1,0:T(8,128)(2,1)S(1)} %bitcast.164, bf16[2048,1024]{1,0:T(8,128)(2,1)S(1)} %get-tuple-element.158), kind=kOutput, calls=%fused_computation.119 | convolution fusion | flops 8589934592 | bytes 16777216 | tf_op jit(solution)/shard_map/dot_general | solution.py:582
  310.7 62.3 %scan_backward.3 = (f32[1280,128]{1,0:T(8,128)}, bf16[1024,1024]{1,0:T(8,128)(2,1)}, f32[128,1024]{1,0:T(8,128)}, f32[1,1024]{1,0:T(1,128)}, f32[16,1024]{1,0:T(8,128)}, /*index=5*/f32[1,1024]{1,0:T(1,128)}) custom-call(s32[4]{0:T(128)} %copy-done.25, s32[2]{0:T(128)} %bitcast.190, f32[1280,128]{1,0:T(8,128)} %convert_add_fusion.5.refs_2_, ...), custom_call_target="tpu_custom_call" | custom-call | tf_op jit(solution)/shard_map/scan_backward/pallas_call | solution.py:322
  382.5 35.5 %scan_backward.2 = (f32[1280,128]{1,0:T(8,128)}, bf16[1024,1024]{1,0:T(8,128)(2,1)}, f32[128,1024]{1,0:T(8,128)}, f32[1,1024]{1,0:T(1,128)}, f32[16,1024]{1,0:T(8,128)}, /*index=5*/f32[1,1024]{1,0:T(1,128)}) custom-call(s32[4]{0:T(128)} %copy-done.25, s32[2]{0:T(128)} %bitcast.191, f32[1280,128]{1,0:T(8,128)} %convert_add_fusion.6.refs_2_, ...), custom_call_target="tpu_custom_call" | custom-call | tf_op jit(solution)/shard_map/scan_backward/pallas_call | solution.py:322
  422.3 13.0 %conv_backward.2 = (bf16[2048,1024]{1,0:T(8,128)(2,1)}, f32[160,1024]{1,0:T(8,128)}, f32[1,1024]{1,0:T(1,128)}, f32[4,1024]{1,0:T(4,128)}) custom-call(s32[4]{0:T(128)} %copy-done.25, s32[2]{0:T(128)} %bitcast.192, f32[1280,128]{1,0:T(8,128)} %convert_add_fusion.4.refs_2_, bf16[1024,1024]{1,0:T(8,128)(2,1)} %get-tuple-element.154.refs_3_, ...), custom_call_target="tpu_custom_call" | custom-call | tf_op jit(solution)/shard_map/conv_backward/pallas_call | solution.py:501
  436.9 15.3 %fusion.38 = f32[2048,2048]{1,0:T(8,128)} fusion(bf16[2048,1024]{1,0:T(8,128)(2,1)} %copy-done.46, bf16[2048,1024]{1,0:T(8,128)(2,1)} %all-gather.5.cloned.1.call-done), kind=kOutput, calls=%fused_computation.120 | convolution fusion | flops 8589934592 | bytes 25165824 | tf_op jit(solution)/shard_map/dot_general | solution.py:582
  453.1 11.7 %conv_backward.3 = (bf16[2048,1024]{1,0:T(8,128)(2,1)}, f32[160,1024]{1,0:T(8,128)}, f32[1,1024]{1,0:T(1,128)}, f32[4,1024]{1,0:T(4,128)}) custom-call(s32[4]{0:T(128)} %copy-done.25, s32[2]{0:T(128)} %bitcast.193, f32[1280,128]{1,0:T(8,128)} %convert_add_fusion.3.refs_2_, ...), custom_call_target="tpu_custom_call", output_to_operand_aliasing={{0}: (10, {})} | custom-call | tf_op jit(solution)/shard_map/conv_backward/pallas_call | solution.py:501
  467.4 14.0 %fusion.39 = bf16[2048,1024]{1,0:T(8,128)(2,1)} fusion(bf16[2048,2048]{1,0:T(8,128)(2,1)} %get-tuple-element.133, bf16[2048,1024]{1,0:T(8,128)(2,1)} %get-tuple-element.179), kind=kOutput, calls=%fused_computation.121 | convolution fusion | flops 8589934592 | bytes 16777216 | tf_op jit(solution)/shard_map/dot_general | solution.py:582
  481.4 15.2 %fusion.40 = f32[2048,2048]{1,0:T(8,128)} fusion(bf16[2048,1024]{1,0:T(8,128)(2,1)} %get-tuple-element.179, bf16[2048,1024]{1,0:T(8,128)(2,1)} %bitcast.159), kind=kOutput, calls=%fused_computation.122 | convolution fusion | flops 8589934592 | bytes 25165824 | tf_op jit(solution)/shard_map/dot_general | solution.py:582
  496.6 11.8 %add_convert_fusion = bf16[2048,2048]{1,0:T(8,128)(2,1)S(1)} fusion(f32[2048,2048]{1,0:T(8,128)} %fusion.38, f32[2048,2048]{1,0:T(8,128)} %fusion.40), kind=kLoop, calls=%fused_computation | loop fusion | flops 8388608 | bytes 41943040 | tf_op jit(solution)/shard_map/convert_element_type | solution.py:709
  514.3 26.5 %collective-permute-start.23 = (bf16[4,311,128]{2,1,0:T(8,128)(2,1)S(1)}, bf16[4,311,128]{2,1,0:T(8,128)(2,1)S(1)}, u32[]{:S(2)}, u32[]{:S(2)}) collective-permute-start(bf16[4,311,128]{2,1,0:T(8,128)(2,1)S(1)} %fusion.23), channel_id=1, source_target_pairs={{0,4},{4,0},{8,12},{12,8},{16,20},{20,16},{24,28},{28,24},{1,5},{5... | collective-permute-start | bytes 955400 | tf_op jit(solution)/shard_map/ppermute | solution.py:575
  548.8 15.5 %collective-permute-start.24 = (bf16[2,311,128]{2,1,0:T(8,128)(2,1)S(1)}, bf16[2,311,128]{2,1,0:T(8,128)(2,1)S(1)}, u32[]{:S(2)}, u32[]{:S(2)}) collective-permute-start(bf16[2,311,128]{2,1,0:T(8,128)(2,1)S(1)} %fusion.26), channel_id=1, source_target_pairs={{0,8},{4,12},{8,0},{12,4},{16,24},{20,28},{24,16},{28,20},{1,9},{5... | collective-permute-start | bytes 477704 | tf_op jit(solution)/shard_map/ppermute | solution.py:575
  568.3 47.0 %collective-permute-start.25 = (bf16[1,311,128]{2,1,0:T(8,128)(2,1)S(1)}, bf16[1,311,128]{2,1,0:T(8,128)(2,1)S(1)}, u32[]{:S(2)}, u32[]{:S(2)}) collective-permute-start(bf16[1,311,128]{2,1,0:T(8,128)(2,1)S(1)} %fusion.29), channel_id=1, source_target_pairs={{0,16},{4,20},{8,24},{12,28},{16,0},{20,4},{24,8},{28,12},{1,17},{... | collective-permute-start | bytes 238856 | tf_op jit(solution)/shard_map/ppermute | solution.py:575
  630.7 29.8 %reduce-scatter.6.cloned.1.call-done = bf16[256,1024]{1,0:T(8,128)(2,1)} async-done(((bf16[2048,1024]{1,0:T(8,128)(2,1)}), bf16[256,1024]{1,0:T(8,128)(2,1)}) %reduce-scatter.6.cloned.1.call-update) | async-done | bytes 524304 | tf_op jit(solution)/shard_map/reduce_scatter | solution.py:707
  (276 shorter events, 174.4 us)
Async XLA Ops:
  17.4 93.0 %all-gather.9.cloned.1.call-start = ((), (), s32[]{:S(2)}) async-start(), calls=%async_computation.12 | async-start | bytes 5455872 | tf_op jit(solution)/shard_map/all_gather | solution.py:617
  27.8 177.4 %all-gather.5.cloned.1.call-start = ((), (), s32[]{:S(2)}) async-start(), calls=%async_computation.7 | async-start | bytes 4718592 | tf_op jit(solution)/shard_map/all_gather | solution.py:623
  28.1 26.1 %collective-permute-start = (bf16[256,2048]{1,0:T(8,128)(2,1)S(1)}, bf16[256,2048]{1,0:T(8,128)(2,1)S(1)}, u32[]{:S(2)}, u32[]{:S(2)}) collective-permute-start(bf16[256,2048]{1,0:T(8,128)(2,1)S(1)} %get-tuple-element.111.refs_2_), channel_id=1, source_target_pairs={{0,2},{1,3},{2,0},{3,1},{4,6},{5,7},{6,4},{7,5},{8,10},{9,11},{10,... | collective-permute-start | bytes 3145736 | tf_op jit(solution)/shard_map/ppermute | solution.py:532
  29.8 46.2 %collective-permute-start.3 = (bf16[256,2048]{1,0:T(8,128)(2,1)S(1)}, bf16[256,2048]{1,0:T(8,128)(2,1)S(1)}, u32[]{:S(2)}, u32[]{:S(2)}) collective-permute-start(bf16[256,2048]{1,0:T(8,128)(2,1)S(1)} %get-tuple-element.121.refs_2_), channel_id=1, source_target_pairs={{0,2},{1,3},{2,0},{3,1},{4,6},{5,7},{6,4},{7,5},{8,10},{9,11},{10,... | collective-permute-start | bytes 3145736 | tf_op jit(solution)/shard_map/ppermute | solution.py:532
  30.2 45.8 %collective-permute-start.1 = (bf16[256,2048]{1,0:T(8,128)(2,1)S(1)}, bf16[256,2048]{1,0:T(8,128)(2,1)S(1)}, u32[]{:S(2)}, u32[]{:S(2)}) collective-permute-start(bf16[256,2048]{1,0:T(8,128)(2,1)S(1)} %get-tuple-element.111.refs_2_), channel_id=1, source_target_pairs={{0,1},{1,0},{2,3},{3,2},{4,5},{5,4},{6,7},{7,6},{8,9},{9,8},{10,11... | collective-permute-start | bytes 3145736 | tf_op jit(solution)/shard_map/ppermute | solution.py:532
  30.2 45.8 %collective-permute-start.4 = (bf16[256,2048]{1,0:T(8,128)(2,1)S(1)}, bf16[256,2048]{1,0:T(8,128)(2,1)S(1)}, u32[]{:S(2)}, u32[]{:S(2)}) collective-permute-start(bf16[256,2048]{1,0:T(8,128)(2,1)S(1)} %get-tuple-element.121.refs_2_), channel_id=1, source_target_pairs={{0,1},{1,0},{2,3},{3,2},{4,5},{5,4},{6,7},{7,6},{8,9},{9,8},{10,11... | collective-permute-start | bytes 3145736 | tf_op jit(solution)/shard_map/ppermute | solution.py:532
  54.2 21.8 %collective-permute-start.2 = (bf16[256,2048]{1,0:T(8,128)(2,1)S(1)}, bf16[256,2048]{1,0:T(8,128)(2,1)S(1)}, u32[]{:S(2)}, u32[]{:S(2)}) collective-permute-start(bf16[256,2048]{1,0:T(8,128)(2,1)S(1)} %collective-permute-done.refs_3_), channel_id=1, source_target_pairs={{0,1},{1,0},{2,3},{3,2},{4,5},{5,4},{6,7},{7,6},{8,9},{9,8},{10,11... | collective-permute-start | bytes 3145736 | tf_op jit(solution)/shard_map/ppermute | solution.py:532
  93.4 163.7 %all-gather.7.cloned.1.call-start = ((), (), s32[]{:S(2)}) async-start(), calls=%async_computation.8 | async-start | bytes 4718592 | tf_op jit(solution)/shard_map/all_gather | solution.py:624
  96.2 47.6 %collective-permute-start.9 = (bf16[2,256,2048]{2,1,0:T(8,128)(2,1)S(1)}, bf16[2,256,2048]{2,1,0:T(8,128)(2,1)}, u32[]{:S(2)}, u32[]{:S(2)}) collective-permute-start(bf16[2,256,2048]{2,1,0:T(8,128)(2,1)S(1)} %fusion.15), channel_id=1, source_target_pairs={{0,2},{1,3},{2,0},{3,1},{4,6},{5,7},{6,4},{7,5},{8,10},{9,11},{10,... | collective-permute-start | bytes 6291464 | tf_op jit(solution)/shard_map/ppermute | solution.py:532
  155.9 226.6 %reduce-scatter.4.cloned.1.call-start = ((), (), s32[]{:S(2)}) async-start(), calls=%async_computation.9 | async-start | bytes 4718592 | tf_op jit(solution)/shard_map/reduce_scatter | solution.py:677
  157.4 63.7 %collective-permute-start.13 = (bf16[2,256,2048]{2,1,0:T(8,128)(2,1)S(1)}, bf16[2,256,2048]{2,1,0:T(8,128)(2,1)}, u32[]{:S(2)}, u32[]{:S(2)}) collective-permute-start(bf16[2,256,2048]{2,1,0:T(8,128)(2,1)S(1)} %fusion.15), channel_id=1, source_target_pairs={{0,1},{1,0},{2,3},{3,2},{4,5},{5,4},{6,7},{7,6},{8,9},{9,8},{10,11... | collective-permute-start | bytes 6291464 | tf_op jit(solution)/shard_map/ppermute | solution.py:532
  157.8 63.4 %collective-permute-start.14 = (bf16[2,256,2048]{2,1,0:T(8,128)(2,1)}, bf16[2,256,2048]{2,1,0:T(8,128)(2,1)}, u32[]{:S(2)}, u32[]{:S(2)}) collective-permute-start(bf16[2,256,2048]{2,1,0:T(8,128)(2,1)} %collective-permute-done.9), channel_id=1, source_target_pairs={{0,1},{1,0},{2,3},{3,2},{4,5},{5,4},{6,7},{7,6},{8,9},{9,8},{10,11... | collective-permute-start | bytes 6291464 | tf_op jit(solution)/shard_map/ppermute | solution.py:532
  160.8 29.4 %collective-permute-start.11 = (bf16[1280,128]{1,0:T(8,128)(2,1)S(1)}, bf16[1280,128]{1,0:T(8,128)(2,1)S(1)}, u32[]{:S(2)}, u32[]{:S(2)}) collective-permute-start(bf16[1280,128]{1,0:T(8,128)(2,1)S(1)} %add_convert_fusion.5), channel_id=1, source_target_pairs={{0,2},{1,3},{2,0},{3,1},{4,6},{5,7},{6,4},{7,5},{8,10},{9,11},{10,... | collective-permute-start | bytes 983048 | tf_op jit(solution)/shard_map/ppermute | solution.py:532
  241.0 377.5 %reduce-scatter.8.cloned.1.call-start = ((), (), s32[]{:S(2)}) async-start(), calls=%async_computation.11 | async-start | bytes 4718592 | tf_op jit(solution)/shard_map/reduce_scatter | solution.py:678
  309.2 68.2 %collective-permute-start.16 = (bf16[512,2048]{1,0:T(8,128)(2,1)S(1)}, bf16[512,2048]{1,0:T(8,128)(2,1)}, u32[]{:S(2)}, u32[]{:S(2)}) collective-permute-start(bf16[512,2048]{1,0:T(8,128)(2,1)S(1)} %slice.191), channel_id=1, source_target_pairs={{0,2},{1,3},{2,0},{3,1},{4,6},{5,7},{6,4},{7,5},{8,10},{9,11},{10,... | collective-permute-start | bytes 6291464 | tf_op jit(solution)/shard_map/ppermute | solution.py:532
  373.3 287.2 %reduce-scatter.6.cloned.1.call-start = ((), (), s32[]{:S(2)}) async-start(), calls=%async_computation.10 | async-start | bytes 4718592 | tf_op jit(solution)/shard_map/reduce_scatter | solution.py:707
  376.7 41.3 %collective-permute-start.19 = (bf16[1280,128]{1,0:T(8,128)(2,1)S(1)}, bf16[1280,128]{1,0:T(8,128)(2,1)S(1)}, u32[]{:S(2)}, u32[]{:S(2)}) collective-permute-start(bf16[1280,128]{1,0:T(8,128)(2,1)S(1)} %add_convert_fusion.3), channel_id=1, source_target_pairs={{0,2},{1,3},{2,0},{3,1},{4,6},{5,7},{6,4},{7,5},{8,10},{9,11},{10,... | collective-permute-start | bytes 983048 | tf_op jit(solution)/shard_map/ppermute | solution.py:532
  417.9 17.3 %collective-permute-start.17 = (f32[1280,128]{1,0:T(8,128)}, f32[1280,128]{1,0:T(8,128)S(1)}, u32[]{:S(2)}, u32[]{:S(2)}) collective-permute-start(f32[1280,128]{1,0:T(8,128)} %get-tuple-element.149), channel_id=1, source_target_pairs={{0,1},{1,0},{2,3},{3,2},{4,5},{5,4},{6,7},{7,6},{8,9},{9,8},{10,11... | collective-permute-start | bytes 1966088 | tf_op jit(solution)/shard_map/ppermute | solution.py:532
  435.4 16.8 %collective-permute-start.20 = (bf16[1280,128]{1,0:T(8,128)(2,1)S(1)}, bf16[1280,128]{1,0:T(8,128)(2,1)S(1)}, u32[]{:S(2)}, u32[]{:S(2)}) collective-permute-start(bf16[1280,128]{1,0:T(8,128)(2,1)S(1)} %add_convert_fusion.4), channel_id=1, source_target_pairs={{0,2},{1,3},{2,0},{3,1},{4,6},{5,7},{6,4},{7,5},{8,10},{9,11},{10,... | collective-permute-start | bytes 983048 | tf_op jit(solution)/shard_map/ppermute | solution.py:532
  513.0 27.8 %collective-permute-start.21 = (bf16[1024,2048]{1,0:T(8,128)(2,1)}, bf16[1024,2048]{1,0:T(8,128)(2,1)}, u32[]{:S(2)}, u32[]{:S(2)}) collective-permute-start(bf16[1024,2048]{1,0:T(8,128)(2,1)} %slice.228), channel_id=1, source_target_pairs={{0,1},{1,0},{2,3},{3,2},{4,5},{5,4},{6,7},{7,6},{8,9},{9,8},{10,11... | collective-permute-start | bytes 12582920 | tf_op jit(solution)/shard_map/ppermute | solution.py:532
  514.3 34.4 %collective-permute-start.23 = (bf16[4,311,128]{2,1,0:T(8,128)(2,1)S(1)}, bf16[4,311,128]{2,1,0:T(8,128)(2,1)S(1)}, u32[]{:S(2)}, u32[]{:S(2)}) collective-permute-start(bf16[4,311,128]{2,1,0:T(8,128)(2,1)S(1)} %fusion.23), channel_id=1, source_target_pairs={{0,4},{4,0},{8,12},{12,8},{16,20},{20,16},{24,28},{28,24},{1,5},{5... | collective-permute-start | bytes 955400 | tf_op jit(solution)/shard_map/ppermute | solution.py:575
  547.7 74.3 %collective-permute-start.22 = (bf16[512,2048]{1,0:T(8,128)(2,1)}, bf16[512,2048]{1,0:T(8,128)(2,1)}, u32[]{:S(2)}, u32[]{:S(2)}) collective-permute-start(bf16[512,2048]{1,0:T(8,128)(2,1)} %slice.230), channel_id=1, source_target_pairs={{0,2},{1,3},{2,0},{3,1},{4,6},{5,7},{6,4},{7,5},{8,10},{9,11},{10,... | collective-permute-start | bytes 6291464 | tf_op jit(solution)/shard_map/ppermute | solution.py:532
  548.8 19.5 %collective-permute-start.24 = (bf16[2,311,128]{2,1,0:T(8,128)(2,1)S(1)}, bf16[2,311,128]{2,1,0:T(8,128)(2,1)S(1)}, u32[]{:S(2)}, u32[]{:S(2)}) collective-permute-start(bf16[2,311,128]{2,1,0:T(8,128)(2,1)S(1)} %fusion.26), channel_id=1, source_target_pairs={{0,8},{4,12},{8,0},{12,4},{16,24},{20,28},{24,16},{28,20},{1,9},{5... | collective-permute-start | bytes 477704 | tf_op jit(solution)/shard_map/ppermute | solution.py:575
  568.3 50.1 %collective-permute-start.25 = (bf16[1,311,128]{2,1,0:T(8,128)(2,1)S(1)}, bf16[1,311,128]{2,1,0:T(8,128)(2,1)S(1)}, u32[]{:S(2)}, u32[]{:S(2)}) collective-permute-start(bf16[1,311,128]{2,1,0:T(8,128)(2,1)S(1)} %fusion.29), channel_id=1, source_target_pairs={{0,16},{4,20},{8,24},{12,28},{16,0},{20,4},{24,8},{28,12},{1,17},{... | collective-permute-start | bytes 238856 | tf_op jit(solution)/shard_map/ppermute | solution.py:575
  (60 other events, 1324.0 us)
Sparse Core Ops, SparseCore 0:
  27.9 82.3 all-gather.8
  112.4 71.1 all-gather.4
  185.7 71.3 all-gather.6
  260.6 87.4 reduce-scatter.3
  373.4 108.1 reduce-scatter.7
  496.7 163.6 reduce-scatter.5
